TPU v7x, 32 devices: a whole 2x2x4 slice. The times are simulated.
32 devices in a mesh: seq: 8 (over y, x, core), fsdp: 4 (over z).
Axes of the slice: x: 2, y: 2, z: 4, core: 2. Of those that a mesh axis runs over, the one named last changes fastest.
Arguments:
- tokens: bfloat16 [16, 1024, 1024], P('fsdp', 'seq'), may hold values from -6 to 6
- pre_gain: bfloat16 [2, 1024], P(None, 'fsdp'), may hold values from 0.5 to 1.5
- in_weight: bfloat16 [2, 1024, 4384], P(None, 'fsdp'), may hold values from -0.1875 to 0.1875
- filter_weight: bfloat16 [2, 4, 2304], P(None, None, 'fsdp'), may hold values from -3 to 3
- filter_bias: bfloat16 [2, 2304], P(None, 'fsdp'), may hold values from -3 to 3
- step_bias: float32 [2, 32], replicated, may hold values from -6 to -2
- decay_log: float32 [2, 32], replicated, may hold values from 0 to 2.77
- skip_scale: float32 [2, 32], replicated, may hold values from 0.5 to 1.5
- inner_gain: bfloat16 [2, 2048], P(None, 'fsdp'), may hold values from 0.5 to 1.5
- out_weight: bfloat16 [2, 2048, 1024], P(None, 'fsdp'), may hold values from -0.125 to 0.125
- cotangent: bfloat16 [16, 1024, 1024], P('fsdp', 'seq'), may hold values from -6 to 6
Outputs:
- output: bfloat16 [16, 1024, 1024], P('fsdp', 'seq')
- token_grad: bfloat16 [16, 1024, 1024], P('fsdp', 'seq')
- pre_gain_grad: float32 [2, 1024], P(None, 'fsdp')
- in_weight_grad: float32 [2, 1024, 4384], P(None, 'fsdp')
- filter_weight_grad: float32 [2, 4, 2304], P(None, None, 'fsdp')
- filter_bias_grad: float32 [2, 2304], P(None, 'fsdp')
- step_bias_grad: float32 [2, 32], replicated
- decay_log_grad: float32 [2, 32], replicated
- skip_scale_grad: float32 [2, 32], replicated
- inner_gain_grad: float32 [2, 2048], P(None, 'fsdp')
- out_weight_grad: float32 [2, 2048, 1024], P(None, 'fsdp')
All inputs are finite; a program needn't handle non-finite values.
Results may differ from a plain program's by a relative error of at most 0.02.
Values may be sent and summed in bfloat16 or wider, within the bound.
A program may use at most 256 MiB of HBM per device.

v0:
```python
import jax
import jax.numpy as jnp
from jax import lax
from jax.sharding import PartitionSpec as P

DI = 2048
NH = 32
HEAD = 64
NS = 128
CONV_K = 4
BLOCK = 256


EPSILON = 1e-05
HIGHEST = lax.Precision.HIGHEST
HALF_TYPE = jnp.bfloat16
FULL_TYPE = jnp.float32


def root_scale(values, gain):
    return values * lax.rsqrt(jnp.mean(values * values, axis=-1, keepdims=True) + EPSILON) * gain


def gated_norm(mixed_rows, gate_rows, gain):
    return root_scale(mixed_rows * jax.nn.silu(gate_rows), gain)


def causal_filter(raw_rows, kernel, offset):
    tap_count = kernel.shape[0]
    length = raw_rows.shape[0]
    padded = jnp.pad(raw_rows, ((tap_count - 1, 0), (0, 0)))
    summed = offset
    for tap_number in range(tap_count):
        summed = summed + padded[tap_number : tap_number + length] * kernel[tap_number]
    return jax.nn.silu(summed)


def head_inputs(
    inner_raw,
    step_raw,
    shared_raw,
    kernel_inner,
    offset_inner,
    kernel_shared,
    offset_shared,
    bias_local,
    decay_local,
):
    inner_filtered = causal_filter(inner_raw, kernel_inner, offset_inner)
    shared_filtered = causal_filter(shared_raw, kernel_shared, offset_shared)
    step_size = jax.nn.softplus(step_raw + bias_local)
    log_rate = -jnp.exp(decay_local) * step_size
    blocks = log_rate.shape[0] // BLOCK
    step_blocks = step_size.reshape(blocks, BLOCK, step_size.shape[1])
    cumulative = jnp.cumsum(log_rate.reshape(blocks, BLOCK, log_rate.shape[1]), axis=1)
    return (inner_filtered, shared_filtered, step_blocks, cumulative)


def mixing(inner_prod, entry_full, exit_full, cumulative, step_blocks):
    cumul_heads = jnp.transpose(cumulative, (0, 2, 1))
    step_heads = jnp.transpose(step_blocks, (0, 2, 1))
    row_index = lax.broadcasted_iota(jnp.int32, (BLOCK, BLOCK), 0)
    column_index = lax.broadcasted_iota(jnp.int32, (BLOCK, BLOCK), 1)
    causal = row_index >= column_index
    spread = cumul_heads[..., :, None] - cumul_heads[..., None, :]
    scores = jnp.where(
        causal, inner_prod * jnp.exp(jnp.where(causal, spread, 0.0)) * step_heads[..., None, :], 0.0
    )
    writes = (jnp.exp(cumul_heads[..., -1:] - cumul_heads) * step_heads)[..., None] * entry_full[
        :, None
    ]
    read_rows = jnp.exp(cumul_heads)[..., None] * exit_full[:, None]
    return (scores, writes, read_rows)


def carry_states(cumulative, states):
    totals = cumulative[:, -1, :]
    running = jnp.cumsum(totals, axis=0)
    before = running - totals
    blocks = totals.shape[0]
    later_mask = (
        lax.broadcasted_iota(jnp.int32, (blocks, blocks), 0)
        > lax.broadcasted_iota(jnp.int32, (blocks, blocks), 1)
    )[..., None]
    block_gaps = before[:, None, :] - running[None, :, :]
    decay_matrix = jnp.where(later_mask, jnp.exp(jnp.where(later_mask, block_gaps, 0.0)), 0.0)
    return jnp.einsum("cdh,dhnp->chnp", decay_matrix, states, precision=HIGHEST)


def split_halves(inner_filtered, shared_filtered, blocks, head_count):
    inner_half = inner_filtered.astype(HALF_TYPE).reshape(blocks, BLOCK, head_count, HEAD)
    shared_half = shared_filtered.astype(HALF_TYPE).reshape(blocks, BLOCK, 2 * NS)
    return (inner_half, shared_half[..., :NS], shared_half[..., NS:])


def head_forward(inner_raw, step_raw, shared_raw, params):
    (
        kernel_inner,
        offset_inner,
        kernel_shared,
        offset_shared,
        bias_local,
        decay_local,
        skip_local,
    ) = params
    inner_filtered, shared_filtered, step_blocks, cumulative = head_inputs(
        inner_raw.astype(FULL_TYPE),
        step_raw.astype(FULL_TYPE),
        shared_raw.astype(FULL_TYPE),
        kernel_inner,
        offset_inner,
        kernel_shared,
        offset_shared,
        bias_local,
        decay_local,
    )
    blocks, head_count = (step_blocks.shape[0], step_blocks.shape[2])
    inner_half, entry_half, exit_half = split_halves(
        inner_filtered, shared_filtered, blocks, head_count
    )
    inner_prod = jnp.einsum("cin,cjn->cij", exit_half, entry_half, preferred_element_type=FULL_TYPE)
    per_head = jnp.broadcast_to(inner_prod[:, None], (blocks, head_count, BLOCK, BLOCK))
    scores, writes, read_rows = mixing(
        per_head, entry_half.astype(FULL_TYPE), exit_half.astype(FULL_TYPE), cumulative, step_blocks
    )
    within = jnp.einsum(
        "chij,cjhp->cihp", scores.astype(HALF_TYPE), inner_half, preferred_element_type=FULL_TYPE
    )
    states = jnp.einsum(
        "chjn,cjhp->chnp", writes.astype(HALF_TYPE), inner_half, preferred_element_type=FULL_TYPE
    )
    carried = carry_states(cumulative, states).astype(HALF_TYPE)
    across = jnp.einsum(
        "chin,chnp->cihp", read_rows.astype(HALF_TYPE), carried, preferred_element_type=FULL_TYPE
    )
    mixed_rows = within + across + skip_local[:, None] * inner_half.astype(FULL_TYPE)
    return mixed_rows.reshape(blocks * BLOCK, head_count * HEAD).astype(HALF_TYPE)


def head_backward(inner_raw, step_raw, shared_raw, mixed_grad, params):
    (
        kernel_inner,
        offset_inner,
        kernel_shared,
        offset_shared,
        bias_local,
        decay_local,
        skip_local,
    ) = params
    prepared, prep_back = jax.vjp(
        head_inputs,
        inner_raw.astype(FULL_TYPE),
        step_raw.astype(FULL_TYPE),
        shared_raw.astype(FULL_TYPE),
        kernel_inner,
        offset_inner,
        kernel_shared,
        offset_shared,
        bias_local,
        decay_local,
    )
    inner_filtered, shared_filtered, step_blocks, cumulative = prepared
    blocks, head_count = (step_blocks.shape[0], step_blocks.shape[2])
    inner_half, entry_half, exit_half = split_halves(
        inner_filtered, shared_filtered, blocks, head_count
    )
    inner_prod = jnp.einsum("cin,cjn->cij", exit_half, entry_half, preferred_element_type=FULL_TYPE)
    per_head = jnp.broadcast_to(inner_prod[:, None], (blocks, head_count, BLOCK, BLOCK))
    mixes, mix_back = jax.vjp(
        mixing,
        per_head,
        entry_half.astype(FULL_TYPE),
        exit_half.astype(FULL_TYPE),
        cumulative,
        step_blocks,
    )
    scores_half = mixes[0].astype(HALF_TYPE)
    writes_half = mixes[1].astype(HALF_TYPE)
    reads_half = mixes[2].astype(HALF_TYPE)
    states = jnp.einsum(
        "chjn,cjhp->chnp", writes_half, inner_half, preferred_element_type=FULL_TYPE
    )
    carried, carry_back = jax.vjp(carry_states, cumulative, states)
    carried_half = carried.astype(HALF_TYPE)
    grad_half = mixed_grad.reshape(blocks, BLOCK, head_count, HEAD)
    grad_full = grad_half.astype(FULL_TYPE)
    skip_grad = jnp.sum(grad_full * inner_half.astype(FULL_TYPE), axis=(0, 1, 3))
    reads_grad = jnp.einsum(
        "cihp,chnp->chin", grad_half, carried_half, preferred_element_type=FULL_TYPE
    )
    carried_grad = jnp.einsum(
        "chin,cihp->chnp", reads_half, grad_half, preferred_element_type=FULL_TYPE
    )
    cumul_grad, states_grad = carry_back(carried_grad)
    states_half = states_grad.astype(HALF_TYPE)
    writes_grad = jnp.einsum(
        "chnp,cjhp->chjn", states_half, inner_half, preferred_element_type=FULL_TYPE
    )
    scores_grad = jnp.einsum(
        "cihp,cjhp->chij", grad_half, inner_half, preferred_element_type=FULL_TYPE
    )
    inner_grad = skip_local[:, None] * grad_full
    inner_grad = inner_grad + jnp.einsum(
        "chjn,chnp->cjhp", writes_half, states_half, preferred_element_type=FULL_TYPE
    )
    inner_grad = inner_grad + jnp.einsum(
        "chij,cihp->cjhp", scores_half, grad_half, preferred_element_type=FULL_TYPE
    )
    prod_grad, entry_grad, exit_grad, cumul_more, step_grad = mix_back(
        (scores_grad, writes_grad, reads_grad)
    )
    prod_half = prod_grad.astype(HALF_TYPE)
    exit_grad = exit_grad + jnp.einsum(
        "chij,cjn->cin", prod_half, entry_half, preferred_element_type=FULL_TYPE
    )
    entry_grad = entry_grad + jnp.einsum(
        "chij,cin->cjn", prod_half, exit_half, preferred_element_type=FULL_TYPE
    )
    length = blocks * BLOCK
    shared_grad = jnp.concatenate([entry_grad, exit_grad], axis=-1).reshape(length, 2 * NS)
    raw_grads = prep_back(
        (
            inner_grad.reshape(length, head_count * HEAD),
            shared_grad,
            step_grad,
            cumul_grad + cumul_more,
        )
    )
    return raw_grads + (skip_grad,)


def per_device(
    tokens,
    pre_gain,
    in_weight,
    filter_weight,
    filter_bias,
    step_bias,
    decay_log,
    skip_scale,
    inner_gain,
    out_weight,
    cotangent,
):
    seq_count = lax.axis_size("seq")
    position = lax.axis_index("seq")
    heads_local = NH // seq_count
    width_local = heads_local * HEAD
    layer_count = in_weight.shape[0]
    residual = tokens.astype(FULL_TYPE)
    saved = []
    for layer_number in range(layer_count):
        weights = (
            lax.all_gather(pre_gain[layer_number], "fsdp", axis=0, tiled=True),
            lax.all_gather(in_weight[layer_number], "fsdp", axis=0, tiled=True),
            lax.all_gather(filter_weight[layer_number], "fsdp", axis=1, tiled=True),
            lax.all_gather(filter_bias[layer_number], "fsdp", axis=0, tiled=True),
            lax.all_gather(inner_gain[layer_number], "fsdp", axis=0, tiled=True),
            lax.all_gather(out_weight[layer_number], "fsdp", axis=0, tiled=True),
        )
        gain_in, weight_in, kernel, offset, gain_mid, weight_out = weights
        normed = root_scale(residual, gain_in.astype(FULL_TYPE)).astype(HALF_TYPE)
        projected = jnp.einsum(
            "gsd,df->gsf", normed, weight_in, preferred_element_type=FULL_TYPE
        ).astype(HALF_TYPE)
        inner_raw = projected[..., DI : 2 * DI]
        shared_raw = projected[..., 2 * DI : 2 * DI + 2 * NS]
        step_raw = projected[..., 2 * DI + 2 * NS :]
        inner_heads, step_heads = (
            lax.all_to_all(inner_raw, "seq", split_axis=2, concat_axis=1, tiled=True),
            lax.all_to_all(step_raw, "seq", split_axis=2, concat_axis=1, tiled=True),
        )
        shared_all = lax.all_gather(shared_raw, "seq", axis=1, tiled=True)
        kernel_full = kernel.astype(FULL_TYPE)
        offset_full = offset.astype(FULL_TYPE)
        params = (
            lax.dynamic_slice_in_dim(kernel_full, position * width_local, width_local, 1),
            lax.dynamic_slice_in_dim(offset_full, position * width_local, width_local, 0),
            kernel_full[:, DI:],
            offset_full[DI:],
            lax.dynamic_slice_in_dim(
                step_bias[layer_number], position * heads_local, heads_local, 0
            ),
            lax.dynamic_slice_in_dim(
                decay_log[layer_number], position * heads_local, heads_local, 0
            ),
            lax.dynamic_slice_in_dim(
                skip_scale[layer_number], position * heads_local, heads_local, 0
            ),
        )
        mixed_heads = lax.map(
            lambda members: head_forward(members[0], members[1], members[2], params),
            (inner_heads, step_heads, shared_all),
        )
        mixed_back = lax.all_to_all(mixed_heads, "seq", split_axis=1, concat_axis=2, tiled=True)
        gated_rows = gated_norm(
            mixed_back.astype(FULL_TYPE),
            projected[..., :DI].astype(FULL_TYPE),
            gain_mid.astype(FULL_TYPE),
        ).astype(HALF_TYPE)
        residual_next = residual + jnp.einsum(
            "gsk,kd->gsd", gated_rows, weight_out, preferred_element_type=FULL_TYPE
        )
        saved.append(
            (
                residual,
                normed,
                projected,
                inner_heads,
                step_heads,
                shared_all,
                mixed_back,
                gated_rows,
                weights,
                params,
            )
        )
        residual = residual_next
    output = residual.astype(HALF_TYPE)
    grad_residual = cotangent.astype(FULL_TYPE)
    head_terms = []
    weight_terms = []
    for layer_number in reversed(range(layer_count)):
        (
            residual,
            normed,
            projected,
            inner_heads,
            step_heads,
            shared_all,
            mixed_back,
            gated_rows,
            weights,
            params,
        ) = saved[layer_number]
        gain_in, weight_in, kernel, offset, gain_mid, weight_out = weights
        branch_grad = grad_residual.astype(HALF_TYPE)
        weight_out_grad = jnp.einsum(
            "gsk,gsd->kd", gated_rows, branch_grad, preferred_element_type=FULL_TYPE
        )
        gated_grad = jnp.einsum(
            "gsd,kd->gsk", branch_grad, weight_out, preferred_element_type=FULL_TYPE
        )
        norm_value, norm_back = jax.vjp(
            gated_norm,
            mixed_back.astype(FULL_TYPE),
            projected[..., :DI].astype(FULL_TYPE),
            gain_mid.astype(FULL_TYPE),
        )
        mixed_grad, gate_grad, gain_mid_grad = norm_back(gated_grad)
        mixed_grad_heads = lax.all_to_all(
            mixed_grad.astype(HALF_TYPE), "seq", split_axis=2, concat_axis=1, tiled=True
        )
        results = lax.map(
            lambda members: head_backward(members[0], members[1], members[2], members[3], params),
            (inner_heads, step_heads, shared_all, mixed_grad_heads),
        )
        (
            inner_grad,
            step_grad,
            shared_grad,
            kernel_inner_grad,
            offset_inner_grad,
            kernel_shared_grad,
            offset_shared_grad,
            bias_grad,
            decay_grad,
            skip_grad,
        ) = results
        inner_back, step_back = (
            lax.all_to_all(
                inner_grad.astype(HALF_TYPE), "seq", split_axis=1, concat_axis=2, tiled=True
            ),
            lax.all_to_all(
                step_grad.astype(HALF_TYPE), "seq", split_axis=1, concat_axis=2, tiled=True
            ),
        )
        shared_back = lax.psum_scatter(
            shared_grad.astype(jnp.bfloat16), "seq", scatter_dimension=1, tiled=True
        ).astype(jnp.float32)
        projected_grad = jnp.concatenate(
            [gate_grad, inner_back.astype(FULL_TYPE), shared_back, step_back.astype(FULL_TYPE)],
            axis=-1,
        ).astype(HALF_TYPE)
        weight_in_grad = jnp.einsum(
            "gsd,gsf->df", normed, projected_grad, preferred_element_type=FULL_TYPE
        )
        normed_grad = jnp.einsum(
            "gsf,df->gsd", projected_grad, weight_in, preferred_element_type=FULL_TYPE
        )
        pre_value, pre_back = jax.vjp(root_scale, residual, gain_in.astype(FULL_TYPE))
        residual_part, gain_in_grad = pre_back(normed_grad)
        grad_residual = grad_residual + residual_part
        kernel_grad = jnp.concatenate(
            [
                lax.dynamic_update_slice_in_dim(
                    jnp.zeros((CONV_K, DI), FULL_TYPE),
                    jnp.sum(kernel_inner_grad, 0),
                    position * width_local,
                    1,
                ),
                jnp.sum(kernel_shared_grad, 0),
            ],
            axis=1,
        )
        offset_grad = jnp.concatenate(
            [
                lax.dynamic_update_slice_in_dim(
                    jnp.zeros((DI,), FULL_TYPE),
                    jnp.sum(offset_inner_grad, 0),
                    position * width_local,
                    0,
                ),
                jnp.sum(offset_shared_grad, 0),
            ],
            axis=0,
        )
        heads_zero = jnp.zeros((NH,), FULL_TYPE)
        head_terms.append(
            tuple(
                (
                    lax.dynamic_update_slice_in_dim(
                        heads_zero, jnp.sum(term_item, 0), position * heads_local, 0
                    )
                    for term_item in (bias_grad, decay_grad, skip_grad)
                )
            )
        )
        sliced = (
            lax.psum_scatter(
                gain_in_grad.astype(jnp.bfloat16), "fsdp", scatter_dimension=0, tiled=True
            ).astype(jnp.float32),
            lax.psum_scatter(
                weight_in_grad.astype(jnp.bfloat16), "fsdp", scatter_dimension=0, tiled=True
            ).astype(jnp.float32),
            lax.psum_scatter(
                kernel_grad.astype(jnp.bfloat16), "fsdp", scatter_dimension=1, tiled=True
            ).astype(jnp.float32),
            lax.psum_scatter(
                offset_grad.astype(jnp.bfloat16), "fsdp", scatter_dimension=0, tiled=True
            ).astype(jnp.float32),
            lax.psum_scatter(
                gain_mid_grad.astype(jnp.bfloat16), "fsdp", scatter_dimension=0, tiled=True
            ).astype(jnp.float32),
            lax.psum_scatter(
                weight_out_grad.astype(jnp.bfloat16), "fsdp", scatter_dimension=0, tiled=True
            ).astype(jnp.float32),
        )
        reduced = (
            lax.psum(sliced[0].astype(jnp.bfloat16), "seq").astype(jnp.float32),
            lax.psum(sliced[1].astype(jnp.bfloat16), "seq").astype(jnp.float32),
            lax.psum(sliced[2].astype(jnp.bfloat16), "seq").astype(jnp.float32),
            lax.psum(sliced[3].astype(jnp.bfloat16), "seq").astype(jnp.float32),
            lax.psum(sliced[4].astype(jnp.bfloat16), "seq").astype(jnp.float32),
            lax.psum(sliced[5].astype(jnp.bfloat16), "seq").astype(jnp.float32),
        )
        weight_terms.append(reduced)
    ordered_weights = weight_terms[::-1]
    ordered_heads = head_terms[::-1]
    bias_stack = jnp.stack([layer_grads[0] for layer_grads in ordered_heads])
    decay_stack = jnp.stack([layer_grads[1] for layer_grads in ordered_heads])
    skip_stack = jnp.stack([layer_grads[2] for layer_grads in ordered_heads])
    bias_total, decay_total, skip_total = lax.psum(
        (bias_stack, decay_stack, skip_stack), ("seq", "fsdp")
    )
    stacked = [
        jnp.stack([layer_grads[member_number] for layer_grads in ordered_weights])
        for member_number in range(6)
    ]
    return (
        output,
        grad_residual.astype(HALF_TYPE),
        stacked[0],
        stacked[1],
        stacked[2],
        stacked[3],
        bias_total,
        decay_total,
        skip_total,
        stacked[4],
        stacked[5],
    )


def solution(mesh):
    in_specs = (
        P("fsdp", "seq", None),
        P(None, "fsdp"),
        P(None, "fsdp", None),
        P(None, None, "fsdp"),
        P(None, "fsdp"),
        P(),
        P(),
        P(),
        P(None, "fsdp"),
        P(None, "fsdp", None),
        P("fsdp", "seq", None),
    )
    out_specs = (
        P("fsdp", "seq", None),
        P("fsdp", "seq", None),
        P(None, "fsdp"),
        P(None, "fsdp", None),
        P(None, None, "fsdp"),
        P(None, "fsdp"),
        P(),
        P(),
        P(),
        P(None, "fsdp"),
        P(None, "fsdp", None),
    )
    return jax.shard_map(
        per_device, mesh=mesh, in_specs=in_specs, out_specs=out_specs, check_vma=False
    )
```

profile of v0, /device:TPU:0, one launch (start us, length us, event | category | flops | bytes accessed | tf_op | source)
XLA Modules:
  0.0 2483.7 jit_solution(13579424342878646557)
XLA Ops:
  12.1 12.6 all-gather.1
  25.6 148.1 %all-gather.23.cloned.1.call-done = bf16[1,1024,4384]{1,2,0:T(8,128)(2,1)} async-done(((bf16[1,256,4384]{1,2,0:T(8,128)(2,1)}), bf16[1,1024,4384]{1,2,0:T(8,128)(2,1)}) %all-gather.23.cloned.1.call-update) | async-done | bytes 8978448 | tf_op jit(solution)/shard_map/all_gather | solution.py:255
  173.7 7.6 fusion.304
  191.7 10.7 copy.764
  209.1 16.5 all-reduce.56
  226.5 38.5 %all-gather.9 = bf16[1,4,2304]{1,0,2:T(2,128)(2,1)S(1)} all-gather(bf16[1,4,576]{1,0,2:T(2,128)(2,1)S(1)} %copy.953), channel_id=11, replica_groups=mesh['seq'=8,'fsdp'=4] {'fsdp'}, dimensions={2}, use_global_device_ids=true | all-gather | bytes 23040 | tf_op jit(solution)/shard_map/all_gather | solution.py:256
  267.5 39.6 %all-gather.3 = bf16[1,4,2304]{1,0,2:T(2,128)(2,1)S(1)} all-gather(bf16[1,4,576]{1,0,2:T(2,128)(2,1)} %copy.952), channel_id=5, replica_groups=mesh['seq'=8,'fsdp'=4] {'fsdp'}, dimensions={2}, use_global_device_ids=true | all-gather | bytes 23040 | tf_op jit(solution)/shard_map/all_gather | solution.py:256
  325.1 99.6 %while.86 = (s32[]{:T(128)}, bf16[4,1024,256]{1,2,0:T(8,128)(2,1)}, f32[256]{0:T(256)S(1)}, bf16[4,1024,256]{1,2,0:T(8,128)(2,1)}, f32[4,256]{1,0:T(4,128)S(1)},...) while((s32[]{:T(128)}, bf16[4,1024,256]{1,2,0:T(8,128)(2,1)}, ...), condition=%wide.region_5.6_spmd, body=%wide.region_1.5_spmd.sunk | while | flops 359936320 | bytes 23048900 | solution.py:291
  433.8 16.7 all-gather.4
  450.5 25.5 %all-gather.7 = bf16[1,1024]{1,0:T(2,128)(2,1)S(1)} all-gather(bf16[1,256]{1,0:T(2,128)(2,1)S(1)} %get-tuple-element.1658), channel_id=9, replica_groups=mesh['seq'=8,'fsdp'=4] {'fsdp'}, dimensions={1}, use_global_device_ids=true | all-gather | bytes 2560 | tf_op jit(solution)/shard_map/all_gather | solution.py:254
  478.9 6.2 multiply_reduce_fusion.33
  485.2 6.0 multiply_reduce_fusion.36
  494.9 7.6 fusion.307
  510.4 10.7 copy.774
  527.7 30.2 %all-to-all-done.3 = bf16[4,128,2048]{1,0,2:T(4,128)(2,1)S(1)} async-done(((bf16[4,128,2048]{1,0,2:T(4,128)(2,1)}), bf16[4,128,2048]{1,0,2:T(4,128)(2,1)S(1)}, u32[]{:S(2)}, u32[]{:S(2)}) %all-to-all-start.3) | async-done | bytes 2097184 | tf_op jit(solution)/shard_map/all_to_all | solution.py:270
  566.4 88.6 %while.87 = (s32[]{:T(128)}, bf16[4,1024,256]{1,2,0:T(8,128)(2,1)}, f32[256]{0:T(256)S(1)}, bf16[4,1024,256]{1,2,0:T(8,128)(2,1)}, f32[4,256]{1,0:T(4,128)S(1)},...) while((s32[]{:T(128)}, bf16[4,1024,256]{1,2,0:T(8,128)(2,1)}, ...), condition=%wide.region_12.13_spmd, body=%wide.region_8.12_spmd.sunk | while | flops 359936320 | bytes 23048900 | solution.py:291
  662.8 22.3 all-gather.10
  692.4 6.4 multiply_reduce_fusion.32
  698.8 7.6 multiply_reduce_fusion.28
  706.5 5.3 fusion.321
  711.8 10.7 copy.785
  726.6 26.1 %all-to-all-done.6 = bf16[4,128,2048]{1,0,2:T(4,128)(2,1)S(1)} async-done(((bf16[4,128,2048]{1,0,2:T(4,128)(2,1)}), bf16[4,128,2048]{1,0,2:T(4,128)(2,1)S(1)}, u32[]{:S(2)}, u32[]{:S(2)}) %all-to-all-start.6) | async-done | bytes 2097184 | tf_op jit(solution)/shard_map/all_to_all | solution.py:351
  767.8 437.2 %while.88 = (s32[]{:T(128)}, bf16[4,1024,256]{2,0,1:T(4,128)(2,1)}, bf16[4,1024,4]{1,2,0:T(4,128)(2,1)}, bf16[4,1024,256]{1,2,0:T(8,128)(2,1)}, f32[4,4,256]{2,1...) while((s32[]{:T(128)}, bf16[4,1024,256]{2,0,1:T(4,128)(2,1)}, ...), condition=%wide.region_47.49_spmd, body=%wide.region_15.48_spmd.sunk | while | flops 879702592 | bytes 136511200 | solution.py:354
  819.3 21.3 dynamic_update_slice.244
  845.7 20.1 reduce-window.129
  928.5 21.3 dynamic_update_slice.244
  954.8 20.1 reduce-window.129
  1037.6 21.3 dynamic_update_slice.244
  1064.0 20.1 reduce-window.129
  1146.8 21.3 dynamic_update_slice.244
  1173.2 20.1 reduce-window.129
  1212.7 7.2 all_to_all.162
  1227.2 29.3 %all-to-all-done.7 = bf16[4,1024,256]{2,0,1:T(4,128)(2,1)} async-done(((bf16[4,1024,256]{2,0,1:T(4,128)(2,1)}), bf16[4,1024,256]{2,0,1:T(4,128)(2,1)}, u32[]{:S(2)}, u32[]{:S(2)}) %all-to-all-start.7) | async-done | bytes 2097184 | tf_op jit(solution)/shard_map/all_to_all | solution.py:371
  1260.8 10.8 reduce-scatter.25.cloned.1.call-done
  1273.0 10.5 multiply_reduce_fusion.34
  1293.9 10.9 copy.793
  1308.4 26.5 %all-to-all-done.9 = bf16[4,128,2048]{1,0,2:T(4,128)(2,1)S(1)} async-done(((bf16[4,128,2048]{1,0,2:T(4,128)(2,1)}), bf16[4,128,2048]{1,0,2:T(4,128)(2,1)S(1)}, u32[]{:S(2)}, u32[]{:S(2)}) %all-to-all-start.9) | async-done | bytes 2097184 | tf_op jit(solution)/shard_map/all_to_all | solution.py:351
  1350.0 439.3 %while.89 = (s32[]{:T(128)}, bf16[4,1024,256]{2,0,1:T(4,128)(2,1)}, bf16[4,1024,4]{1,2,0:T(4,128)(2,1)}, bf16[4,1024,256]{1,2,0:T(8,128)(2,1)}, f32[4,4,256]{2,1...) while((s32[]{:T(128)}, bf16[4,1024,256]{2,0,1:T(4,128)(2,1)}, ...), condition=%wide.region_83.85_spmd, body=%wide.region_51.84_spmd.sunk | while | flops 879702592 | bytes 136236144 | solution.py:354
  1402.5 21.3 dynamic_update_slice.254
  1428.9 20.1 reduce-window.133
  1512.2 21.3 dynamic_update_slice.254
  1538.6 20.1 reduce-window.133
  1621.9 21.3 dynamic_update_slice.254
  1648.3 20.1 reduce-window.133
  1731.6 21.3 dynamic_update_slice.254
  1758.0 20.1 reduce-window.133
  1794.4 6.1 bitcast_convert_fusion.10
  1802.2 6.4 bitcast_convert_fusion.11
  1810.2 9.6 bitcast_convert_fusion.8
  1823.3 7.2 all_to_all.163
  1840.2 21.4 all-to-all-done.10
  1867.8 9.7 bitcast_convert_fusion.9
  1882.6 31.8 %reduce-scatter.23.cloned.1.call-done = bf16[512,1024]{1,0:T(8,128)(2,1)} async-done(((bf16[2048,1024]{1,0:T(8,128)(2,1)}), bf16[512,1024]{1,0:T(8,128)(2,1)}) %reduce-scatter.23.cloned.1.call-update) | async-done | bytes 1048592 | tf_op jit(solution)/shard_map/reduce_scatter | solution.py:445
  1914.4 79.5 %reduce-scatter.21.cloned.1.call-done = bf16[512,1024]{1,0:T(8,128)(2,1)} async-done(((bf16[2048,1024]{1,0:T(8,128)(2,1)}), bf16[512,1024]{1,0:T(8,128)(2,1)}) %reduce-scatter.21.cloned.1.call-update) | async-done | bytes 1048592 | tf_op jit(solution)/shard_map/reduce_scatter | solution.py:445
  1994.0 157.3 %reduce-scatter.19.cloned.1.call-done = bf16[256,4384]{0,1:T(8,128)(2,1)} async-done(((bf16[1024,4384]{0,1:T(8,128)(2,1)}), bf16[256,4384]{0,1:T(8,128)(2,1)}) %reduce-scatter.19.cloned.1.call-update) | async-done | bytes 2244624 | tf_op jit(solution)/shard_map/reduce_scatter | solution.py:433
  2151.3 157.0 %reduce-scatter.17.cloned.1.call-done = bf16[256,4384]{0,1:T(8,128)(2,1)} async-done(((bf16[1024,4384]{0,1:T(8,128)(2,1)}), bf16[256,4384]{0,1:T(8,128)(2,1)}) %reduce-scatter.17.cloned.1.call-update) | async-done | bytes 2244624 | tf_op jit(solution)/shard_map/reduce_scatter | solution.py:433
  2308.4 6.9 add_convert_fusion
  2316.2 17.9 reduce-scatter.31.cloned.1.call-done
  2336.0 39.3 %all-reduce.52 = (f32[2,32]{1,0:T(2,128)}, f32[2,32]{1,0:T(2,128)}, f32[2,32]{1,0:T(2,128)}) all-reduce(f32[2,32]{1,0:T(2,128)S(1)} %pad_maximum_fusion.12, f32[2,32]{1,0:T(2,128)S(1)} %pad_maximum_fusion.13, f32[2,32]{1,0:T(2,128)S(1)} %pad_maximum_fusion.14), channel_id=1, replica_groups=mesh['seq'=8,'fsdp'=4] {'seq','fsdp'}, use_global_device_ids=true, to_apply=%region_114.116 | all-reduce | flops 192 | bytes 1536 | tf_op jit(solution)/shard_map/psum | solution.py:463
  2376.5 11.1 fusion.333
  2387.6 17.9 all-reduce.55
  2406.0 22.8 all-reduce.53
  2434.4 33.6 %all-reduce.59.cloned.1.call-done = (bf16[1,256,4384]{1,2,0:T(8,128)(2,1)}, bf16[1,256,4384]{1,2,0:T(8,128)(2,1)}, bf16[1,512,1024]{2,1,0:T(8,128)(2,1)}, bf16[1,512,1024]{2,1,0:T(8,128)(2,1)}) async-done(((bf16[1,256,4384]{1,2,0:T(8,128)(2,1)}, bf16[1,256,4384]{1,2,0:T(8,128)(2,1)}, bf16[1,512,1024]{2,1,0:T(8,128)(2,1)}, bf16[1,512,1024]{2,1,0:T(8,128)(2,1)}), (bf16[1,256,4384]{1,2,0:T(8,128)(2,1)}, ...) | async-done | bytes 6586384 | tf_op jit(solution)/shard_map/psum | solution.py:451
  2468.0 6.6 maximum_convert_fusion
  (2084 shorter events, 933.6 us)
Async XLA Ops:
  7.2 166.5 %all-gather.23.cloned.1.call-start = ((), (), s32[]{:S(2)}) async-start(), calls=%async_computation.26 | async-start | bytes 11223040 | tf_op jit(solution)/shard_map/all_gather | solution.py:255
  12.1 311.5 %all-gather.19.cloned.1.call-start = ((), (), s32[]{:S(2)}) async-start(), calls=%async_computation.20 | async-start | bytes 2359296 | tf_op jit(solution)/shard_map/all_gather | solution.py:273
  24.8 156.5 %copy-start.144 = (f32[1,1024]{1,0:T(1,128)}, f32[1,1024]{1,0:T(1,128)S(1)}, u32[]{:S(2)}) copy-start(f32[1,1024]{1,0:T(1,128)S(1)} %convert_element_type.808) | copy-start | bytes 12292
  25.6 155.7 %copy-start.156 = (f32[4,128]{1,0:T(4,128)}, f32[4,128]{1,0:T(4,128)S(1)}, u32[]{:S(2)}) copy-start(f32[4,128]{1,0:T(4,128)S(1)} %fusion.347) | copy-start | bytes 6148
  184.2 301.0 %all-gather.25.cloned.1.call-start = ((), (), s32[]{:S(2)}) async-start(), calls=%async_computation.27 | async-start | bytes 5242880 | tf_op jit(solution)/shard_map/all_gather | solution.py:259
  188.0 14.4 all-to-all-start.1
  202.4 114.2 %all-to-all-start = ((bf16[4,128,2048]{1,0,2:T(4,128)(2,1)}), bf16[4,128,2048]{1,0,2:T(4,128)(2,1)S(1)}, u32[]{:S(2)}, u32[]{:S(2)}) async-start(bf16[4,128,2048]{1,0,2:T(4,128)(2,1)} %copy.764), calls=%async_computation | async-start | bytes 4194304 | tf_op jit(solution)/shard_map/all_to_all | solution.py:270
  206.8 288.2 %all-gather.27.cloned.1.call-start = ((), (), s32[]{:S(2)}) async-start(), calls=%async_computation.28 | async-start | bytes 11223040 | tf_op jit(solution)/shard_map/all_gather | solution.py:255
  266.3 53.1 %copy-start.46 = (f32[1,4,2304]{1,0,2:T(1,128)}, f32[1,4,2304]{1,0,2:T(1,128)S(1)}, u32[]{:S(2)}) copy-start(f32[1,4,2304]{1,0,2:T(1,128)S(1)} %convert_element_type.813) | copy-start | bytes 110596
  429.1 46.9 %all-to-all-start.2 = ((bf16[4,1024,256]{2,0,1:T(4,128)(2,1)}), bf16[4,1024,256]{2,0,1:T(4,128)(2,1)S(1)}, u32[]{:S(2)}, u32[]{:S(2)}) async-start(bf16[4,1024,256]{2,0,1:T(4,128)(2,1)} %copy.771), calls=%async_computation.2 | async-start | bytes 4194304 | tf_op jit(solution)/shard_map/all_to_all | solution.py:295
  433.7 131.0 %all-gather.21.cloned.1.call-start = ((), (), s32[]{:S(2)}) async-start(), calls=%async_computation.21 | async-start | bytes 2359296 | tf_op jit(solution)/shard_map/all_gather | solution.py:273
  450.5 34.7 %copy-start.100 = (f32[1,2048]{1,0:T(1,128)}, f32[1,2048]{1,0:T(1,128)S(1)}, u32[]{:S(2)}) copy-start(f32[1,2048]{1,0:T(1,128)S(1)} %convert_element_type.810) | copy-start | bytes 24580
  507.0 14.1 all-to-all-start.4
  521.1 36.8 %all-to-all-start.3 = ((bf16[4,128,2048]{1,0,2:T(4,128)(2,1)}), bf16[4,128,2048]{1,0,2:T(4,128)(2,1)S(1)}, u32[]{:S(2)}, u32[]{:S(2)}) async-start(bf16[4,128,2048]{1,0,2:T(4,128)(2,1)} %copy.774), calls=%async_computation.3 | async-start | bytes 4194304 | tf_op jit(solution)/shard_map/all_to_all | solution.py:270
  525.2 173.6 %all-gather.29.cloned.1.call-start = ((), (), s32[]{:S(2)}) async-start(), calls=%async_computation.29 | async-start | bytes 5242880 | tf_op jit(solution)/shard_map/all_gather | solution.py:259
  659.2 30.2 %all-to-all-start.5 = ((bf16[4,1024,256]{2,0,1:T(4,128)(2,1)}), bf16[4,1024,256]{2,0,1:T(4,128)(2,1)S(1)}, u32[]{:S(2)}, u32[]{:S(2)}) async-start(bf16[4,1024,256]{2,0,1:T(4,128)(2,1)} %copy.781), calls=%async_computation.5 | async-start | bytes 4194304 | tf_op jit(solution)/shard_map/all_to_all | solution.py:295
  722.5 30.2 %all-to-all-start.6 = ((bf16[4,128,2048]{1,0,2:T(4,128)(2,1)}), bf16[4,128,2048]{1,0,2:T(4,128)(2,1)S(1)}, u32[]{:S(2)}, u32[]{:S(2)}) async-start(bf16[4,128,2048]{1,0,2:T(4,128)(2,1)} %copy.785), calls=%async_computation.6 | async-start | bytes 4194304 | tf_op jit(solution)/shard_map/all_to_all | solution.py:351
  726.1 545.5 %reduce-scatter.25.cloned.1.call-start = ((), (), s32[]{:S(2)}) async-start(), calls=%async_computation.30 | async-start | bytes 2359296
  817.5 28.1 %copy-start.59 = (f32[4,4,256]{2,1,0:T(4,128)S(1)}, f32[4,4,256]{2,1,0:T(4,128)}, u32[]{:S(2)}) copy-start(f32[4,4,256]{2,1,0:T(4,128)} %get-tuple-element.2295) | copy-start | bytes 49156 | tf_op jit(solution)/shard_map/while
  817.5 50.2 %copy-start.2 = (f32[1024,256]{0,1:T(8,128)S(1)}, f32[1024,256]{0,1:T(8,128)}, u32[]{:S(2)}) copy-start(f32[1024,256]{0,1:T(8,128)} %get-tuple-element.2301) | copy-start | bytes 3145732 | tf_op jit(solution)/shard_map/while
  817.5 50.2 %copy-start.79 = (f32[1,256]{1,0:T(1,128)S(1)}, f32[1,256]{1,0:T(1,128)}, u32[]{:S(2)}) copy-start(f32[1,256]{1,0:T(1,128)} %copy-done.78) | copy-start | bytes 3076 | tf_op jit(solution)/shard_map/while
  926.7 28.1 %copy-start.59 = (f32[4,4,256]{2,1,0:T(4,128)S(1)}, f32[4,4,256]{2,1,0:T(4,128)}, u32[]{:S(2)}) copy-start(f32[4,4,256]{2,1,0:T(4,128)} %get-tuple-element.2295) | copy-start | bytes 49156 | tf_op jit(solution)/shard_map/while
  926.7 28.1 %copy-start.61 = (f32[4,4,256]{2,1,0:T(4,128)S(1)}, f32[4,4,256]{2,1,0:T(4,128)}, u32[]{:S(2)}) copy-start(f32[4,4,256]{2,1,0:T(4,128)} %get-tuple-element.2292) | copy-start | bytes 49156 | tf_op jit(solution)/shard_map/while
  926.7 50.2 %copy-start.2 = (f32[1024,256]{0,1:T(8,128)S(1)}, f32[1024,256]{0,1:T(8,128)}, u32[]{:S(2)}) copy-start(f32[1024,256]{0,1:T(8,128)} %get-tuple-element.2301) | copy-start | bytes 3145732 | tf_op jit(solution)/shard_map/while
  926.7 50.2 %copy-start.79 = (f32[1,256]{1,0:T(1,128)S(1)}, f32[1,256]{1,0:T(1,128)}, u32[]{:S(2)}) copy-start(f32[1,256]{1,0:T(1,128)} %copy-done.78) | copy-start | bytes 3076 | tf_op jit(solution)/shard_map/while
  1035.8 28.1 %copy-start.59 = (f32[4,4,256]{2,1,0:T(4,128)S(1)}, f32[4,4,256]{2,1,0:T(4,128)}, u32[]{:S(2)}) copy-start(f32[4,4,256]{2,1,0:T(4,128)} %get-tuple-element.2295) | copy-start | bytes 49156 | tf_op jit(solution)/shard_map/while
  1035.9 50.2 %copy-start.2 = (f32[1024,256]{0,1:T(8,128)S(1)}, f32[1024,256]{0,1:T(8,128)}, u32[]{:S(2)}) copy-start(f32[1024,256]{0,1:T(8,128)} %get-tuple-element.2301) | copy-start | bytes 3145732 | tf_op jit(solution)/shard_map/while
  1035.9 50.2 %copy-start.79 = (f32[1,256]{1,0:T(1,128)S(1)}, f32[1,256]{1,0:T(1,128)}, u32[]{:S(2)}) copy-start(f32[1,256]{1,0:T(1,128)} %copy-done.78) | copy-start | bytes 3076 | tf_op jit(solution)/shard_map/while
  1145.0 28.1 %copy-start.59 = (f32[4,4,256]{2,1,0:T(4,128)S(1)}, f32[4,4,256]{2,1,0:T(4,128)}, u32[]{:S(2)}) copy-start(f32[4,4,256]{2,1,0:T(4,128)} %get-tuple-element.2295) | copy-start | bytes 49156 | tf_op jit(solution)/shard_map/while
  1145.0 50.2 %copy-start.2 = (f32[1024,256]{0,1:T(8,128)S(1)}, f32[1024,256]{0,1:T(8,128)}, u32[]{:S(2)}) copy-start(f32[1024,256]{0,1:T(8,128)} %get-tuple-element.2301) | copy-start | bytes 3145732 | tf_op jit(solution)/shard_map/while
  1145.0 50.2 %copy-start.79 = (f32[1,256]{1,0:T(1,128)S(1)}, f32[1,256]{1,0:T(1,128)}, u32[]{:S(2)}) copy-start(f32[1,256]{1,0:T(1,128)} %copy-done.78) | copy-start | bytes 3076 | tf_op jit(solution)/shard_map/while
  1219.9 36.6 %all-to-all-start.7 = ((bf16[4,1024,256]{2,0,1:T(4,128)(2,1)}), bf16[4,1024,256]{2,0,1:T(4,128)(2,1)}, u32[]{:S(2)}, u32[]{:S(2)}) async-start(bf16[4,1024,256]{2,0,1:T(4,128)(2,1)} %get-tuple-element.999), calls=%async_computation.7 | async-start | bytes 4194304 | tf_op jit(solution)/shard_map/all_to_all | solution.py:371
  1224.2 48.7 %copy-start.27 = (f32[4,128,1024]{2,1,0:T(8,128)S(1)}, f32[4,128,1024]{2,1,0:T(8,128)}, u32[]{:S(2)}) copy-start(f32[4,128,1024]{2,1,0:T(8,128)} %copy-done.26) | copy-start | bytes 6291460
  1224.2 48.7 %copy-start.147 = (f32[1,1024]{1,0:T(1,128)S(1)}, f32[1,1024]{1,0:T(1,128)}, u32[]{:S(2)}) copy-start(f32[1,1024]{1,0:T(1,128)} %copy-done.146) | copy-start | bytes 12292
  1224.3 48.7 %copy-start.159 = (f32[4,128]{1,0:T(4,128)S(1)}, f32[4,128]{1,0:T(4,128)}, u32[]{:S(2)}) copy-start(f32[4,128]{1,0:T(4,128)} %copy-done.158) | copy-start | bytes 6148
  1227.2 56.3 %copy-start.136 = (bf16[4,8,128,4]{2,3,1,0:T(4,128)(2,1)}, bf16[4,8,128,4]{2,3,1,0:T(4,128)(2,1)S(1)}, u32[]{:S(2)}) copy-start(bf16[4,8,128,4]{2,3,1,0:T(4,128)(2,1)S(1)} %copy.791) | copy-start | bytes 98308
  1304.8 30.2 %all-to-all-start.9 = ((bf16[4,128,2048]{1,0,2:T(4,128)(2,1)}), bf16[4,128,2048]{1,0,2:T(4,128)(2,1)S(1)}, u32[]{:S(2)}, u32[]{:S(2)}) async-start(bf16[4,128,2048]{1,0,2:T(4,128)(2,1)} %copy.793), calls=%async_computation.9 | async-start | bytes 4194304 | tf_op jit(solution)/shard_map/all_to_all | solution.py:351
  1308.4 557.4 %reduce-scatter.27.cloned.1.call-start = ((), (), s32[]{:S(2)}) async-start(), calls=%async_computation.31 | async-start | bytes 2359296
  1400.7 28.1 %copy-start.60 = (f32[4,4,256]{2,1,0:T(4,128)S(1)}, f32[4,4,256]{2,1,0:T(4,128)}, u32[]{:S(2)}) copy-start(f32[4,4,256]{2,1,0:T(4,128)} %get-tuple-element.2376) | copy-start | bytes 49156 | tf_op jit(solution)/shard_map/while
  1400.7 50.2 %copy-start.3 = (f32[1024,256]{0,1:T(8,128)S(1)}, f32[1024,256]{0,1:T(8,128)}, u32[]{:S(2)}) copy-start(f32[1024,256]{0,1:T(8,128)} %get-tuple-element.2382) | copy-start | bytes 3145732 | tf_op jit(solution)/shard_map/while
  1400.8 50.2 %copy-start.81 = (f32[1,256]{1,0:T(1,128)S(1)}, f32[1,256]{1,0:T(1,128)}, u32[]{:S(2)}) copy-start(f32[1,256]{1,0:T(1,128)} %copy-done.80) | copy-start | bytes 3076 | tf_op jit(solution)/shard_map/while
  1510.4 28.1 %copy-start.60 = (f32[4,4,256]{2,1,0:T(4,128)S(1)}, f32[4,4,256]{2,1,0:T(4,128)}, u32[]{:S(2)}) copy-start(f32[4,4,256]{2,1,0:T(4,128)} %get-tuple-element.2376) | copy-start | bytes 49156 | tf_op jit(solution)/shard_map/while
  1510.4 50.2 %copy-start.3 = (f32[1024,256]{0,1:T(8,128)S(1)}, f32[1024,256]{0,1:T(8,128)}, u32[]{:S(2)}) copy-start(f32[1024,256]{0,1:T(8,128)} %get-tuple-element.2382) | copy-start | bytes 3145732 | tf_op jit(solution)/shard_map/while
  1510.4 50.2 %copy-start.81 = (f32[1,256]{1,0:T(1,128)S(1)}, f32[1,256]{1,0:T(1,128)}, u32[]{:S(2)}) copy-start(f32[1,256]{1,0:T(1,128)} %copy-done.80) | copy-start | bytes 3076 | tf_op jit(solution)/shard_map/while
  1620.1 28.1 %copy-start.60 = (f32[4,4,256]{2,1,0:T(4,128)S(1)}, f32[4,4,256]{2,1,0:T(4,128)}, u32[]{:S(2)}) copy-start(f32[4,4,256]{2,1,0:T(4,128)} %get-tuple-element.2376) | copy-start | bytes 49156 | tf_op jit(solution)/shard_map/while
  1620.1 50.2 %copy-start.3 = (f32[1024,256]{0,1:T(8,128)S(1)}, f32[1024,256]{0,1:T(8,128)}, u32[]{:S(2)}) copy-start(f32[1024,256]{0,1:T(8,128)} %get-tuple-element.2382) | copy-start | bytes 3145732 | tf_op jit(solution)/shard_map/while
  1620.1 50.2 %copy-start.81 = (f32[1,256]{1,0:T(1,128)S(1)}, f32[1,256]{1,0:T(1,128)}, u32[]{:S(2)}) copy-start(f32[1,256]{1,0:T(1,128)} %copy-done.80) | copy-start | bytes 3076 | tf_op jit(solution)/shard_map/while
  1729.8 28.1 %copy-start.60 = (f32[4,4,256]{2,1,0:T(4,128)S(1)}, f32[4,4,256]{2,1,0:T(4,128)}, u32[]{:S(2)}) copy-start(f32[4,4,256]{2,1,0:T(4,128)} %get-tuple-element.2376) | copy-start | bytes 49156 | tf_op jit(solution)/shard_map/while
  1729.8 50.2 %copy-start.3 = (f32[1024,256]{0,1:T(8,128)S(1)}, f32[1024,256]{0,1:T(8,128)}, u32[]{:S(2)}) copy-start(f32[1024,256]{0,1:T(8,128)} %get-tuple-element.2382) | copy-start | bytes 3145732 | tf_op jit(solution)/shard_map/while
  1729.8 50.2 %copy-start.81 = (f32[1,256]{1,0:T(1,128)S(1)}, f32[1,256]{1,0:T(1,128)}, u32[]{:S(2)}) copy-start(f32[1,256]{1,0:T(1,128)} %copy-done.80) | copy-start | bytes 3076 | tf_op jit(solution)/shard_map/while
  1794.3 120.2 %reduce-scatter.23.cloned.1.call-start = ((), (), s32[]{:S(2)}) async-start(), calls=%async_computation.25 | async-start | bytes 5242880 | tf_op jit(solution)/shard_map/reduce_scatter | solution.py:445
  1800.5 193.4 %reduce-scatter.21.cloned.1.call-start = ((), (), s32[]{:S(2)}) async-start(), calls=%async_computation.24 | async-start | bytes 5242880 | tf_op jit(solution)/shard_map/reduce_scatter | solution.py:445
  1808.7 342.6 %reduce-scatter.19.cloned.1.call-start = ((), (), s32[]{:S(2)}) async-start(), calls=%async_computation.23 | async-start | bytes 11223040 | tf_op jit(solution)/shard_map/reduce_scatter | solution.py:433
  1830.5 31.0 %all-to-all-start.10 = ((bf16[4,1024,256]{2,0,1:T(4,128)(2,1)}), bf16[4,1024,256]{2,0,1:T(4,128)(2,1)}, u32[]{:S(2)}, u32[]{:S(2)}) async-start(bf16[4,1024,256]{2,0,1:T(4,128)(2,1)} %get-tuple-element.2746), calls=%async_computation.10 | async-start | bytes 4194304 | tf_op jit(solution)/shard_map/all_to_all | solution.py:371
  1834.9 33.0 %copy-start.37 = (bf16[4,128,1024]{2,1,0:T(8,128)(2,1)S(1)}, bf16[4,128,1024]{2,1,0:T(8,128)(2,1)}, u32[]{:S(2)}) copy-start(bf16[4,128,1024]{2,1,0:T(8,128)(2,1)} %param.20) | copy-start | bytes 3145732
  1834.9 33.0 %copy-start.145 = (f32[1,1024]{1,0:T(1,128)S(1)}, f32[1,1024]{1,0:T(1,128)}, u32[]{:S(2)}) copy-start(f32[1,1024]{1,0:T(1,128)} %copy-done.144) | copy-start | bytes 12292
  1834.9 32.9 %copy-start.157 = (f32[4,128]{1,0:T(4,128)S(1)}, f32[4,128]{1,0:T(4,128)}, u32[]{:S(2)}) copy-start(f32[4,128]{1,0:T(4,128)} %copy-done.156) | copy-start | bytes 6148
  1834.9 473.3 %reduce-scatter.17.cloned.1.call-start = ((), (), s32[]{:S(2)}) async-start(), calls=%async_computation.22 | async-start | bytes 11223040 | tf_op jit(solution)/shard_map/reduce_scatter | solution.py:433
  1877.5 456.5 %reduce-scatter.31.cloned.1.call-start = ((), (), s32[]{:S(2)}) async-start(), calls=%async_computation.33 | async-start | bytes 737280
  1879.4 496.0 %reduce-scatter.29.cloned.1.call-start = ((), (), s32[]{:S(2)}) async-start(), calls=%async_computation.32 | async-start | bytes 737280
  1880.7 587.3 %all-reduce.59.cloned.1.call-start = ((), (), s32[]{:S(2)}) async-start(), calls=%async_computation.34 | async-start | bytes 13172736 | tf_op jit(solution)/shard_map/psum | solution.py:451
  2308.4 68.0 %copy-start.77 = (bf16[4,128,256]{1,2,0:T(8,128)(2,1)S(1)}, bf16[4,128,256]{1,2,0:T(8,128)(2,1)}, u32[]{:S(2)}) copy-start(bf16[4,128,256]{1,2,0:T(8,128)(2,1)} %copy.841) | copy-start | bytes 786436
  2376.4 54.8 %copy-start.139 = (f32[4,128]{1,0:T(4,128)S(1)}, f32[4,128]{1,0:T(4,128)}, u32[]{:S(2)}) copy-start(f32[4,128]{1,0:T(4,128)} %copy-done.138) | copy-start | bytes 6148
  2376.4 54.8 %copy-start.44 = (f32[4,128,1024]{2,1,0:T(8,128)S(1)}, f32[4,128,1024]{2,1,0:T(8,128)}, u32[]{:S(2)}) copy-start(f32[4,128,1024]{2,1,0:T(8,128)} %copy-done.42) | copy-start | bytes 6291460
  (405 other events, 3873.4 us)
Sparse Core Ops, SparseCore 0:
  12.2 161.4 all-gather.22
  184.3 26.4 all-gather.18
  212.9 120.3 all-gather.24
  334.7 160.1 all-gather.26
  505.6 51.4 all-gather.20
  559.1 85.7 all-gather.28
  1210.0 61.4 reduce-scatter.24
  1794.4 40.3 reduce-scatter.26
  1837.6 76.7 reduce-scatter.22
  1916.7 77.2 reduce-scatter.20
  1996.9 154.2 reduce-scatter.18
  2153.5 154.7 reduce-scatter.16
  2311.1 22.9 reduce-scatter.30
  2336.2 20.2 reduce-scatter.28
  2360.1 107.7 all-reduce.58
where the time goes:
time: 2510 us; the launch traced here: 2480 us
  waiting for transfers between devices  778 us (31%)
  local copies, waits for them, and re-layouts  551 us (22%)
  other arithmetic  486 us (19%)
  matrix products  335 us (13%)
  blocking collectives  266 us (11%)
  starting transfers between devices  41 us (2%)
    reduce_scatter x2, waiting for transfers between devices, per_device(): lax.psum_scatter(weight_in_grad.astype(jnp.bfloat16), 'fsdp', scatter_dim...  314 us
    another operation x90, other arithmetic  254 us
    dynamic_update_slice x64, local copies, waits for them, and re-layouts, per_device(): lax.map(lambda members: head_backward(members[0], members[1], members[2],...  234 us
    all_gather x2, waiting for transfers between devices, per_device(): lax.all_gather(in_weight[layer_number], 'fsdp', axis=0, tiled=True)  152 us
    reduce_scatter x2, waiting for transfers between devices, per_device(): lax.psum_scatter(weight_out_grad.astype(jnp.bfloat16), 'fsdp', scatter_di...  111 us
    all_gather x2, blocking collectives, per_device(): lax.all_gather(filter_weight[layer_number], 'fsdp', axis=1, tiled=True)  78.1 us
    dot_general x32, matrix products, carry_states(): return jnp.einsum('cdh,dhnp->chnp', decay_matrix, states, precision=HIGHEST)  75.8 us
    all_to_all x2, waiting for transfers between devices, per_device(): lax.all_to_all(mixed_grad.astype(HALF_TYPE), 'seq', split_axis=2, concat_...  52.6 us
  transfers between devices with their start and end apart: 25, of which 15 were waited for; matrix products, arithmetic and copies ran while one was open for 14% of the time, Pallas kernels for 0%

commit v1 on v0

v1 whole, which is shorter than its diff:
```python
import jax
import jax.numpy as jnp
from jax import lax
from jax.sharding import Mesh
from jax.sharding import PartitionSpec as P

DI = 2048
NH = 32
HEAD = 64
NS = 128
CONV_K = 4
BLOCK = 256


EPSILON = 1e-05
HIGHEST = lax.Precision.HIGHEST
HALF_TYPE = jnp.bfloat16
FULL_TYPE = jnp.float32


def root_scale(values, gain):
    return values * lax.rsqrt(jnp.mean(values * values, axis=-1, keepdims=True) + EPSILON) * gain


def gated_norm(mixed_rows, gate_rows, gain):
    return root_scale(mixed_rows * jax.nn.silu(gate_rows), gain)


def causal_filter(raw_rows, kernel, offset):
    tap_count = kernel.shape[0]
    length = raw_rows.shape[0]
    padded = jnp.pad(raw_rows, ((tap_count - 1, 0), (0, 0)))
    summed = offset
    for tap_number in range(tap_count):
        summed = summed + padded[tap_number : tap_number + length] * kernel[tap_number]
    return jax.nn.silu(summed)


def head_inputs(
    inner_raw,
    step_raw,
    shared_raw,
    kernel_inner,
    offset_inner,
    kernel_shared,
    offset_shared,
    bias_local,
    decay_local,
):
    inner_filtered = causal_filter(inner_raw, kernel_inner, offset_inner)
    shared_filtered = causal_filter(shared_raw, kernel_shared, offset_shared)
    step_size = jax.nn.softplus(step_raw + bias_local)
    log_rate = -jnp.exp(decay_local) * step_size
    blocks = log_rate.shape[0] // BLOCK
    step_blocks = step_size.reshape(blocks, BLOCK, step_size.shape[1])
    rate_blocks = log_rate.reshape(blocks, BLOCK, log_rate.shape[1])
    lower = jnp.tri(BLOCK, dtype=FULL_TYPE)
    cumulative = jnp.einsum("ij,cjh->cih", lower, rate_blocks, precision=HIGHEST)
    return (inner_filtered, shared_filtered, step_blocks, cumulative)


def mixing(inner_prod, entry_full, exit_full, cumulative, step_blocks):
    cumul_heads = jnp.transpose(cumulative, (0, 2, 1))
    step_heads = jnp.transpose(step_blocks, (0, 2, 1))
    row_index = lax.broadcasted_iota(jnp.int32, (BLOCK, BLOCK), 0)
    column_index = lax.broadcasted_iota(jnp.int32, (BLOCK, BLOCK), 1)
    causal = row_index >= column_index
    spread = cumul_heads[..., :, None] - cumul_heads[..., None, :]
    scores = jnp.where(
        causal, inner_prod[:, None] * jnp.exp(jnp.where(causal, spread, 0.0)) * step_heads[..., None, :], 0.0
    )
    writes = (jnp.exp(cumul_heads[..., -1:] - cumul_heads) * step_heads)[..., None] * entry_full[
        :, None
    ]
    read_rows = jnp.exp(cumul_heads)[..., None] * exit_full[:, None]
    return (scores, writes, read_rows)


def carry_states(cumulative, states):
    totals = jnp.exp(cumulative[:, -1, :])
    carried = jnp.zeros_like(states[0])
    entering = []
    for block_number in range(states.shape[0]):
        entering.append(carried)
        carried = totals[block_number][:, None, None] * carried + states[block_number]
    return jnp.stack(entering)


def split_halves(inner_filtered, shared_filtered, blocks, head_count):
    inner_half = inner_filtered.astype(HALF_TYPE).reshape(blocks, BLOCK, head_count, HEAD)
    shared_half = shared_filtered.astype(HALF_TYPE).reshape(blocks, BLOCK, 2 * NS)
    return (inner_half, shared_half[..., :NS], shared_half[..., NS:])


def head_forward(inner_raw, step_raw, shared_raw, params):
    (
        kernel_inner,
        offset_inner,
        kernel_shared,
        offset_shared,
        bias_local,
        decay_local,
        skip_local,
    ) = params
    inner_filtered, shared_filtered, step_blocks, cumulative = head_inputs(
        inner_raw.astype(FULL_TYPE),
        step_raw.astype(FULL_TYPE),
        shared_raw.astype(FULL_TYPE),
        kernel_inner,
        offset_inner,
        kernel_shared,
        offset_shared,
        bias_local,
        decay_local,
    )
    blocks, head_count = (step_blocks.shape[0], step_blocks.shape[2])
    inner_half, entry_half, exit_half = split_halves(
        inner_filtered, shared_filtered, blocks, head_count
    )
    inner_prod = jnp.einsum("cin,cjn->cij", exit_half, entry_half, preferred_element_type=FULL_TYPE)
    scores, writes, read_rows = mixing(
        inner_prod, entry_half.astype(FULL_TYPE), exit_half.astype(FULL_TYPE), cumulative, step_blocks
    )
    within = jnp.einsum(
        "chij,cjhp->cihp", scores.astype(HALF_TYPE), inner_half, preferred_element_type=FULL_TYPE
    )
    states = jnp.einsum(
        "chjn,cjhp->chnp", writes.astype(HALF_TYPE), inner_half, preferred_element_type=FULL_TYPE
    )
    carried = carry_states(cumulative, states).astype(HALF_TYPE)
    across = jnp.einsum(
        "chin,chnp->cihp", read_rows.astype(HALF_TYPE), carried, preferred_element_type=FULL_TYPE
    )
    mixed_rows = within + across + skip_local[:, None] * inner_half.astype(FULL_TYPE)
    return mixed_rows.reshape(blocks * BLOCK, head_count * HEAD).astype(HALF_TYPE)


def head_backward(inner_raw, step_raw, shared_raw, mixed_grad, params):
    (
        kernel_inner,
        offset_inner,
        kernel_shared,
        offset_shared,
        bias_local,
        decay_local,
        skip_local,
    ) = params
    prepared, prep_back = jax.vjp(
        head_inputs,
        inner_raw.astype(FULL_TYPE),
        step_raw.astype(FULL_TYPE),
        shared_raw.astype(FULL_TYPE),
        kernel_inner,
        offset_inner,
        kernel_shared,
        offset_shared,
        bias_local,
        decay_local,
    )
    inner_filtered, shared_filtered, step_blocks, cumulative = prepared
    blocks, head_count = (step_blocks.shape[0], step_blocks.shape[2])
    inner_half, entry_half, exit_half = split_halves(
        inner_filtered, shared_filtered, blocks, head_count
    )
    inner_prod = jnp.einsum("cin,cjn->cij", exit_half, entry_half, preferred_element_type=FULL_TYPE)
    mixes, mix_back = jax.vjp(
        mixing,
        inner_prod,
        entry_half.astype(FULL_TYPE),
        exit_half.astype(FULL_TYPE),
        cumulative,
        step_blocks,
    )
    scores_half = mixes[0].astype(HALF_TYPE)
    writes_half = mixes[1].astype(HALF_TYPE)
    reads_half = mixes[2].astype(HALF_TYPE)
    states = jnp.einsum(
        "chjn,cjhp->chnp", writes_half, inner_half, preferred_element_type=FULL_TYPE
    )
    carried, carry_back = jax.vjp(carry_states, cumulative, states)
    carried_half = carried.astype(HALF_TYPE)
    grad_half = mixed_grad.reshape(blocks, BLOCK, head_count, HEAD)
    grad_full = grad_half.astype(FULL_TYPE)
    skip_grad = jnp.sum(grad_full * inner_half.astype(FULL_TYPE), axis=(0, 1, 3))
    reads_grad = jnp.einsum(
        "cihp,chnp->chin", grad_half, carried_half, preferred_element_type=FULL_TYPE
    )
    carried_grad = jnp.einsum(
        "chin,cihp->chnp", reads_half, grad_half, preferred_element_type=FULL_TYPE
    )
    cumul_grad, states_grad = carry_back(carried_grad)
    states_half = states_grad.astype(HALF_TYPE)
    writes_grad = jnp.einsum(
        "chnp,cjhp->chjn", states_half, inner_half, preferred_element_type=FULL_TYPE
    )
    scores_grad = jnp.einsum(
        "cihp,cjhp->chij", grad_half, inner_half, preferred_element_type=FULL_TYPE
    )
    inner_grad = skip_local[:, None] * grad_full
    inner_grad = inner_grad + jnp.einsum(
        "chjn,chnp->cjhp", writes_half, states_half, preferred_element_type=FULL_TYPE
    )
    inner_grad = inner_grad + jnp.einsum(
        "chij,cihp->cjhp", scores_half, grad_half, preferred_element_type=FULL_TYPE
    )
    prod_grad, entry_grad, exit_grad, cumul_more, step_grad = mix_back(
        (scores_grad, writes_grad, reads_grad)
    )
    prod_half = prod_grad.astype(HALF_TYPE)
    exit_grad = exit_grad + jnp.einsum(
        "cij,cjn->cin", prod_half, entry_half, preferred_element_type=FULL_TYPE
    )
    entry_grad = entry_grad + jnp.einsum(
        "cij,cin->cjn", prod_half, exit_half, preferred_element_type=FULL_TYPE
    )
    length = blocks * BLOCK
    shared_grad = jnp.concatenate([entry_grad, exit_grad], axis=-1).reshape(length, 2 * NS)
    raw_grads = prep_back(
        (
            inner_grad.reshape(length, head_count * HEAD),
            shared_grad,
            step_grad,
            cumul_grad + cumul_more,
        )
    )
    return raw_grads + (skip_grad,)


def gather_rows(shard):
    parts = lax.axis_size("chip") * lax.axis_size("core")
    part_rows = shard.shape[0] // parts
    part_number = lax.axis_index("chip") * lax.axis_size("core") + lax.axis_index("core")
    part = lax.dynamic_slice_in_dim(shard, part_number * part_rows, part_rows, 0)
    return lax.all_gather(part, ("fsdp", "chip", "core"), axis=0, tiled=True)


def scatter_rows(total):
    fsdp_count = lax.axis_size("fsdp")
    chips, cores = (lax.axis_size("chip"), lax.axis_size("core"))
    rows, columns = total.shape
    part_rows = rows // (fsdp_count * chips * cores)
    half = total.astype(HALF_TYPE)
    part = lax.psum_scatter(half, ("fsdp", "chip", "core"), scatter_dimension=0, tiled=True)
    return lax.all_gather(part, ("chip", "core"), axis=0, tiled=True)


def per_device(
    tokens,
    pre_gain,
    in_weight,
    filter_weight,
    filter_bias,
    step_bias,
    decay_log,
    skip_scale,
    inner_gain,
    out_weight,
    cotangent,
):
    core_count = lax.axis_size("core")
    position = lax.axis_index("core")
    fsdp_count = lax.axis_size("fsdp")
    heads_local = NH // core_count
    width_local = heads_local * HEAD
    layer_count = in_weight.shape[0]
    small_parts = (pre_gain, filter_weight, filter_bias, inner_gain)
    small_flat = jnp.concatenate([part.reshape(-1) for part in small_parts])
    small_all = lax.all_gather(small_flat, "fsdp", axis=0)
    small_full = []
    start = 0
    for part in small_parts:
        piece = small_all[:, start : start + part.size].reshape((fsdp_count,) + part.shape)
        start += part.size
        piece = jnp.moveaxis(piece, 0, -2)
        small_full.append(piece.reshape(part.shape[:-1] + (-1,)))
    weights_in = []
    weights_out = []
    for layer_number in range(layer_count):
        weights_in.append(gather_rows(in_weight[layer_number]))
        weights_out.append(gather_rows(out_weight[layer_number]))
    residual = lax.all_to_all(tokens, "chip", split_axis=0, concat_axis=0, tiled=True)
    cotangent = lax.all_to_all(cotangent, "chip", split_axis=0, concat_axis=0, tiled=True)
    residual = residual.astype(FULL_TYPE)
    chunks, chunk_rows = residual.shape[:2]
    length = chunks * core_count * chunk_rows
    saved = []
    for layer_number in range(layer_count):
        gain_in, kernel, offset, gain_mid = [part[layer_number] for part in small_full]
        weight_in = weights_in[layer_number]
        weight_out = weights_out[layer_number]
        normed = root_scale(residual, gain_in.astype(FULL_TYPE)).astype(HALF_TYPE)
        projected = jnp.einsum(
            "gsd,df->gsf", normed, weight_in, preferred_element_type=FULL_TYPE
        ).astype(HALF_TYPE)
        inner_raw = projected[..., DI : 2 * DI]
        inner_heads = lax.all_to_all(inner_raw, "core", split_axis=2, concat_axis=1, tiled=True)
        inner_heads = inner_heads.reshape(length, width_local)
        extra_all = lax.all_gather(projected[..., 2 * DI :], "core", axis=1, tiled=True)
        extra_all = extra_all.reshape(length, 2 * NS + NH)
        shared_all = extra_all[:, : 2 * NS]
        step_heads = lax.dynamic_slice_in_dim(
            extra_all, 2 * NS + position * heads_local, heads_local, 1
        )
        kernel_full = kernel.astype(FULL_TYPE)
        offset_full = offset.astype(FULL_TYPE)
        params = (
            lax.dynamic_slice_in_dim(kernel_full, position * width_local, width_local, 1),
            lax.dynamic_slice_in_dim(offset_full, position * width_local, width_local, 0),
            kernel_full[:, DI:],
            offset_full[DI:],
            lax.dynamic_slice_in_dim(
                step_bias[layer_number], position * heads_local, heads_local, 0
            ),
            lax.dynamic_slice_in_dim(
                decay_log[layer_number], position * heads_local, heads_local, 0
            ),
            lax.dynamic_slice_in_dim(
                skip_scale[layer_number], position * heads_local, heads_local, 0
            ),
        )
        mixed_heads = head_forward(inner_heads, step_heads, shared_all, params)
        mixed_heads = mixed_heads.reshape(chunks, core_count * chunk_rows, width_local)
        mixed_back = lax.all_to_all(mixed_heads, "core", split_axis=1, concat_axis=2, tiled=True)
        gated_rows = gated_norm(
            mixed_back.astype(FULL_TYPE),
            projected[..., :DI].astype(FULL_TYPE),
            gain_mid.astype(FULL_TYPE),
        ).astype(HALF_TYPE)
        residual_next = residual + jnp.einsum(
            "gsk,kd->gsd", gated_rows, weight_out, preferred_element_type=FULL_TYPE
        )
        saved.append(
            (
                residual,
                normed,
                projected,
                inner_heads,
                step_heads,
                shared_all,
                mixed_back,
                gated_rows,
                (gain_in, weight_in, gain_mid, weight_out),
                params,
            )
        )
        residual = residual_next
    output = residual.astype(HALF_TYPE)
    grad_residual = cotangent.astype(FULL_TYPE)
    small_terms = []
    in_terms = []
    out_terms = []
    for layer_number in reversed(range(layer_count)):
        (
            residual,
            normed,
            projected,
            inner_heads,
            step_heads,
            shared_all,
            mixed_back,
            gated_rows,
            weights,
            params,
        ) = saved[layer_number]
        gain_in, weight_in, gain_mid, weight_out = weights
        branch_grad = grad_residual.astype(HALF_TYPE)
        gated_grad = jnp.einsum(
            "gsd,kd->gsk", branch_grad, weight_out, preferred_element_type=FULL_TYPE
        )
        norm_value, norm_back = jax.vjp(
            gated_norm,
            mixed_back.astype(FULL_TYPE),
            projected[..., :DI].astype(FULL_TYPE),
            gain_mid.astype(FULL_TYPE),
        )
        mixed_grad, gate_grad, gain_mid_grad = norm_back(gated_grad)
        mixed_grad_heads = lax.all_to_all(
            mixed_grad.astype(HALF_TYPE), "core", split_axis=2, concat_axis=1, tiled=True
        ).reshape(length, width_local)
        weight_out_grad = jnp.einsum(
            "gsk,gsd->kd", gated_rows, branch_grad, preferred_element_type=FULL_TYPE
        )
        out_terms.append(scatter_rows(weight_out_grad))
        (
            inner_grad,
            step_grad,
            shared_grad,
            kernel_inner_grad,
            offset_inner_grad,
            kernel_shared_grad,
            offset_shared_grad,
            bias_grad,
            decay_grad,
            skip_grad,
        ) = head_backward(inner_heads, step_heads, shared_all, mixed_grad_heads, params)
        inner_back = lax.all_to_all(
            inner_grad.astype(HALF_TYPE).reshape(chunks, core_count * chunk_rows, width_local),
            "core",
            split_axis=1,
            concat_axis=2,
            tiled=True,
        )
        step_wide = lax.dynamic_update_slice_in_dim(
            jnp.zeros((length, NH), HALF_TYPE),
            step_grad.astype(HALF_TYPE),
            position * heads_local,
            1,
        )
        extra_grad = jnp.concatenate([shared_grad.astype(HALF_TYPE), step_wide], axis=1)
        extra_back = lax.psum_scatter(
            extra_grad.reshape(chunks, core_count * chunk_rows, 2 * NS + NH),
            "core",
            scatter_dimension=1,
            tiled=True,
        )
        projected_grad = jnp.concatenate(
            [gate_grad.astype(HALF_TYPE), inner_back, extra_back], axis=-1
        )
        weight_in_grad = jnp.einsum(
            "gsd,gsf->df", normed, projected_grad, preferred_element_type=FULL_TYPE
        )
        in_terms.append(scatter_rows(weight_in_grad))
        normed_grad = jnp.einsum(
            "gsf,df->gsd", projected_grad, weight_in, preferred_element_type=FULL_TYPE
        )
        pre_value, pre_back = jax.vjp(root_scale, residual, gain_in.astype(FULL_TYPE))
        residual_part, gain_in_grad = pre_back(normed_grad)
        grad_residual = grad_residual + residual_part
        kernel_grad = jnp.concatenate(
            [
                lax.dynamic_update_slice_in_dim(
                    jnp.zeros((CONV_K, DI), FULL_TYPE),
                    kernel_inner_grad,
                    position * width_local,
                    1,
                ),
                kernel_shared_grad,
            ],
            axis=1,
        )
        offset_grad = jnp.concatenate(
            [
                lax.dynamic_update_slice_in_dim(
                    jnp.zeros((DI,), FULL_TYPE),
                    offset_inner_grad,
                    position * width_local,
                    0,
                ),
                offset_shared_grad,
            ],
            axis=0,
        )
        heads_zero = jnp.zeros((NH,), FULL_TYPE)
        head_grads = [
            lax.dynamic_update_slice_in_dim(heads_zero, term_item, position * heads_local, 0)
            for term_item in (bias_grad, decay_grad, skip_grad)
        ]
        small_terms.append([gain_in_grad, kernel_grad, offset_grad, gain_mid_grad] + head_grads)
    layer_order = list(reversed(range(layer_count)))
    small_shapes = [item.shape for item in small_terms[0]]
    small_vector = jnp.concatenate(
        [item.reshape(-1) for number in layer_order for item in small_terms[number]]
    )
    small_rows = lax.psum(small_vector, ("chip", "core", "fsdp")).reshape(layer_count, -1)
    small_totals = []
    start = 0
    for shape in small_shapes:
        size = 1
        for extent in shape:
            size *= extent
        small_totals.append(small_rows[:, start : start + size].reshape((layer_count,) + shape))
        start += size
    shard_number = lax.axis_index("fsdp")
    for member_number in range(4):
        member = small_totals[member_number]
        width = member.shape[-1] // fsdp_count
        small_totals[member_number] = lax.dynamic_slice_in_dim(
            member, shard_number * width, width, member.ndim - 1
        )
    gain_in_total, kernel_total, offset_total, gain_mid_total = small_totals[:4]
    bias_total, decay_total, skip_total = small_totals[4:]
    output = lax.all_to_all(output, "chip", split_axis=0, concat_axis=0, tiled=True)
    token_grad = lax.all_to_all(
        grad_residual.astype(HALF_TYPE), "chip", split_axis=0, concat_axis=0, tiled=True
    )
    return (
        output,
        token_grad,
        gain_in_total,
        jnp.stack([in_terms[number] for number in layer_order]).astype(FULL_TYPE),
        kernel_total,
        offset_total,
        bias_total,
        decay_total,
        skip_total,
        gain_mid_total,
        jnp.stack([out_terms[number] for number in layer_order]).astype(FULL_TYPE),
    )


def solution(mesh):
    seq_count = mesh.shape["seq"]
    fsdp_count = mesh.shape["fsdp"]
    seq_spec = ("chip", "core")

    def whole(*arrays):
        chips = arrays[0].shape[0] // fsdp_count
        grid = mesh.devices.reshape(chips, seq_count // chips, fsdp_count)
        fine_mesh = Mesh(grid, ("chip", "core", "fsdp"))
        in_specs = (
            P("fsdp", seq_spec, None),
            P(None, "fsdp"),
            P(None, "fsdp", None),
            P(None, None, "fsdp"),
            P(None, "fsdp"),
            P(),
            P(),
            P(),
            P(None, "fsdp"),
            P(None, "fsdp", None),
            P("fsdp", seq_spec, None),
        )
        out_specs = (
            P("fsdp", seq_spec, None),
            P("fsdp", seq_spec, None),
            P(None, "fsdp"),
            P(None, "fsdp", None),
            P(None, None, "fsdp"),
            P(None, "fsdp"),
            P(),
            P(),
            P(),
            P(None, "fsdp"),
            P(None, "fsdp", None),
        )
        return jax.shard_map(
            per_device, mesh=fine_mesh, in_specs=in_specs, out_specs=out_specs, check_vma=False
        )(*arrays)

    return whole
```

time: 2510 us -> 1450 us (0.58)
  other arithmetic: 486 us -> 148 us
  local copies, waits for them, and re-layouts: 551 us -> 238 us
  blocking collectives: 266 us -> 64.7 us
  matrix products: 335 us -> 199 us
    another operation x123 -> x6, other arithmetic: 266 us -> 13.5 us  [whole(): jax.shard_map(per_device, mesh=fine_mesh, in_specs=in_specs, out_specs=ou...]
    dynamic_update_slice x82 -> x8, local copies, waits for them, and re-layouts: 242 us -> 2.28 us  [the longest x4 1.53 us: per_device(): lax.dynamic_update_slice_in_dim(heads_zero, term_item, position * heads_l...]
    all_gather x6 -> x3, blocking collectives: 155 us -> 18.6 us  [the longest x1 13.8 us: per_device(): small_all = lax.all_gather(small_flat, 'fsdp', axis=0)]
    all_to_all x10 -> x4, waiting for transfers between devices: 138 us -> 6.14 us  [the longest x1 6.13 us: per_device(): lax.all_to_all(output, 'chip', split_axis=0, concat_axis=0, tiled=True)]
    dot_general x64 -> x8, matrix products: 96.2 us -> 9.04 us  [the longest x2 3.2 us: head_backward(): jnp.einsum('cij,cin->cjn', prod_half, exit_half, preferred_element_type=F...]
    psum x1, waiting for transfers between devices: 33.6 us -> 103 us  [per_device(): lax.psum(small_vector, ('chip', 'core', 'fsdp')).reshape(layer_count, -1)]
    psum x2 -> x0, blocking collectives: 62.2 us -> none  [the longest x1 39.3 us: per_device(): lax.psum((bias_stack, decay_stack, skip_stack), ('seq', 'fsdp'))]
    all_gather x6 -> x8, waiting for transfers between devices: 152 us -> 196 us  [the longest x4 101 us: scatter_rows(): return lax.all_gather(part, ('chip', 'core'), axis=0, tiled=True)]
  transfers between devices with their start and end apart: 25 -> 19, of which waited for: 15 -> 12; matrix products, arithmetic and copies ran while one was open for 14% -> 27% of each run, Pallas kernels for 0% -> 0%
where the time goes in v1:
time: 1450 us; the launch traced here: 1440 us
  waiting for transfers between devices  758 us (52%)
  local copies, waits for them, and re-layouts  238 us (16%)
  matrix products  199 us (14%)
  other arithmetic  148 us (10%)
  blocking collectives  64.7 us (4%)
  starting transfers between devices  17.2 us (1%)
  between operations  17.1 us (1%)
    reduce_scatter x4, waiting for transfers between devices, scatter_rows(): lax.psum_scatter(half, ('fsdp', 'chip', 'core'), scatter_dimension=0, til...  453 us
    psum x1, waiting for transfers between devices, per_device(): lax.psum(small_vector, ('chip', 'core', 'fsdp')).reshape(layer_count, -1)  103 us
    all_gather x4, waiting for transfers between devices, scatter_rows(): return lax.all_gather(part, ('chip', 'core'), axis=0, tiled=True)  101 us
    all_gather x4, waiting for transfers between devices, gather_rows(): return lax.all_gather(part, ('fsdp', 'chip', 'core'), axis=0, tiled=True)  94.6 us
    unnamed x411, local copies, waits for them, and re-layouts  33.9 us
    reshape x4, local copies, waits for them, and re-layouts, head_backward(): inner_grad.reshape(length, head_count * HEAD)  32.1 us
    reduce_sum x4, other arithmetic, causal_filter(): padded[tap_number:tap_number + length] * kernel[tap_number]  29.1 us
  transfers between devices with their start and end apart: 19, of which 12 were waited for; matrix products, arithmetic and copies ran while one was open for 27% of the time, Pallas kernels for 0%

profile of v1, /device:TPU:0, one launch (start us, length us, event | category | flops | bytes accessed | tf_op | source)
XLA Modules:
  0.0 1442.2 jit_solution(12104981775829278998)
XLA Ops:
  18.9 5.2 all-to-all-start
  26.0 13.8 all-gather.5
  44.0 59.4 %all-gather.23.cloned.1.call-done = bf16[1,1024,4384]{2,1,0:T(8,128)(2,1)} async-done(((bf16[1,32,4384]{2,1,0:T(8,128)(2,1)}), bf16[1,1024,4384]{2,1,0:T(8,128)(2,1)}) %all-gather.23.cloned.1.call-update) | async-done | bytes 8978448 | tf_op jit(solution)/shard_map/all_gather | solution.py:234
  103.4 7.9 fusion.14
  123.9 9.7 copy.341
  133.7 5.7 all_to_all.122
  141.9 5.4 copy.343
  147.3 9.3 multiply_convert_fusion.17
  160.5 5.8 copy.350
  187.2 5.9 all_to_all.123
  196.2 5.4 copy.359
  201.6 6.2 multiply_reduce_fusion.26
  207.8 6.0 multiply_reduce_fusion.29
  213.9 35.2 %all-gather.27.cloned.1.call-done = bf16[1,1024,4384]{2,1,0:T(8,128)(2,1)} async-done(((bf16[1,32,4384]{2,1,0:T(8,128)(2,1)}), bf16[1,1024,4384]{2,1,0:T(8,128)(2,1)}) %all-gather.27.cloned.1.call-update) | async-done | bytes 8978448 | tf_op jit(solution)/shard_map/all_gather | solution.py:234
  249.1 7.9 fusion.17
  257.2 9.9 copy.363
  267.2 5.4 all_to_all.124
  275.1 5.5 copy.365
  280.7 8.9 multiply_convert_fusion.15
  293.5 5.9 copy.371
  322.7 6.6 all_to_all.125
  336.7 5.7 copy.380
  342.4 6.2 multiply_reduce_fusion.25
  348.7 7.9 fusion.50
  360.9 9.7 copy.382
  370.6 5.6 all_to_all.126
  384.5 13.9 fusion.11
  405.7 6.2 fusion.22
  439.0 5.8 bitcast_add_fusion.2
  444.7 8.5 copy.470
  453.2 7.6 reshape.693
  460.8 10.9 multiply_reduce_fusion.15
  471.7 5.9 broadcast_multiply_fusion
  477.6 5.6 fusion.49
  484.9 5.6 all_to_all.127
  498.1 10.9 multiply_reduce_fusion.27
  519.8 9.7 copy.410
  529.5 5.8 all_to_all.128
  544.9 14.0 fusion.13
  590.0 6.9 bitcast_convert_fusion.2
  597.5 7.2 bitcast_convert_fusion.3
  605.8 11.2 bitcast_convert_fusion
  618.5 5.7 fusion.20
  627.6 8.5 copy.473
  636.1 7.6 reshape.694
  643.7 11.2 multiply_reduce_fusion.21
  655.0 5.9 broadcast_multiply_fusion.4
  660.9 5.6 fusion.48
  668.2 5.6 all_to_all.129
  678.7 11.2 bitcast_convert_fusion.1
  711.7 12.2 fusion.80
  725.6 16.8 %reduce-scatter.17.cloned.1.call-done = bf16[64,1024]{1,0:T(8,128)(2,1)} async-done(((bf16[2048,1024]{1,0:T(8,128)(2,1)}), bf16[64,1024]{1,0:T(8,128)(2,1)}) %reduce-scatter.17.cloned.1.call-update) | async-done | bytes 131088 | tf_op jit(solution)/shard_map/reduce_scatter | solution.py:243
  742.5 138.9 %reduce-scatter.15.cloned.1.call-done = bf16[64,1024]{1,0:T(8,128)(2,1)} async-done(((bf16[2048,1024]{1,0:T(8,128)(2,1)}), bf16[64,1024]{1,0:T(8,128)(2,1)}) %reduce-scatter.15.cloned.1.call-update) | async-done | bytes 131088 | tf_op jit(solution)/shard_map/reduce_scatter | solution.py:243
  881.5 148.8 %reduce-scatter.13.cloned.1.call-done = bf16[32,4384]{1,0:T(8,128)(2,1)} async-done(((bf16[1024,4384]{1,0:T(8,128)(2,1)}), bf16[32,4384]{1,0:T(8,128)(2,1)}) %reduce-scatter.13.cloned.1.call-update) | async-done | bytes 280592 | tf_op jit(solution)/shard_map/reduce_scatter | solution.py:243
  1030.4 148.5 %reduce-scatter.11.cloned.1.call-done = bf16[32,4384]{1,0:T(8,128)(2,1)} async-done(((bf16[1024,4384]{1,0:T(8,128)(2,1)}), bf16[32,4384]{1,0:T(8,128)(2,1)}) %reduce-scatter.11.cloned.1.call-update) | async-done | bytes 280592 | tf_op jit(solution)/shard_map/reduce_scatter | solution.py:243
  1178.9 6.9 add_convert_fusion.2
  1193.1 6.1 all-to-all-done.5
  1202.8 103.0 %all-reduce.54.cloned.1.call-done = f32[2,14688]{1,0:T(2,128)} async-done(((f32[2,14688]{1,0:T(2,128)}), f32[2,14688]{1,0:T(2,128)}) %all-reduce.54.cloned.1.call-update) | async-done | bytes 117520 | tf_op jit(solution)/shard_map/psum | solution.py:464
  1312.9 18.4 %all-gather.21.cloned.1.call-done = bf16[512,1024]{1,0:T(8,128)(2,1)} async-done(((bf16[64,1024]{1,0:T(8,128)(2,1)}), bf16[512,1024]{1,0:T(8,128)(2,1)}) %all-gather.21.cloned.1.call-update) | async-done | bytes 1048592 | tf_op jit(solution)/shard_map/all_gather | solution.py:244
  1331.3 25.4 %all-gather.19.cloned.1.call-done = bf16[512,1024]{1,0:T(8,128)(2,1)} async-done(((bf16[64,1024]{1,0:T(8,128)(2,1)}), bf16[512,1024]{1,0:T(8,128)(2,1)}) %all-gather.19.cloned.1.call-update) | async-done | bytes 1048592 | tf_op jit(solution)/shard_map/all_gather | solution.py:244
  1360.5 26.7 %all-gather.17.cloned.1.call-done = bf16[256,4384]{1,0:T(8,128)(2,1)} async-done(((bf16[32,4384]{1,0:T(8,128)(2,1)}), bf16[256,4384]{1,0:T(8,128)(2,1)}) %all-gather.17.cloned.1.call-update) | async-done | bytes 2244624 | tf_op jit(solution)/shard_map/all_gather | solution.py:244
  1387.2 30.5 %all-gather.15.cloned.1.call-done = bf16[256,4384]{1,0:T(8,128)(2,1)} async-done(((bf16[32,4384]{1,0:T(8,128)(2,1)}), bf16[256,4384]{1,0:T(8,128)(2,1)}) %all-gather.15.cloned.1.call-update) | async-done | bytes 2244624 | tf_op jit(solution)/shard_map/all_gather | solution.py:244
  1417.7 6.5 maximum_convert_fusion
  1424.2 9.3 copy.442
  (679 shorter events, 264.0 us)
Async XLA Ops:
  7.2 96.2 %all-gather.23.cloned.1.call-start = ((), (), s32[]{:S(2)}) async-start(), calls=%async_computation.27 | async-start | bytes 9461760 | tf_op jit(solution)/shard_map/all_gather | solution.py:234
  13.9 193.9 %all-gather.25.cloned.1.call-start = ((), (), s32[]{:S(2)}) async-start(), calls=%async_computation.28 | async-start | bytes 4325376 | tf_op jit(solution)/shard_map/all_gather | solution.py:234
  16.7 24.1 %copy-start.184 = (f32[2,32]{1,0:T(2,128)S(1)}, f32[2,32]{1,0:T(2,128)}, u32[]{:S(2)}) copy-start(f32[2,32]{1,0:T(2,128)} %param.18) | copy-start | bytes 772
  16.7 24.1 %copy-start.185 = (f32[2,32]{1,0:T(2,128)S(1)}, f32[2,32]{1,0:T(2,128)}, u32[]{:S(2)}) copy-start(f32[2,32]{1,0:T(2,128)} %param.17) | copy-start | bytes 772
  16.7 24.1 %copy-start.186 = (f32[2,32]{1,0:T(2,128)S(1)}, f32[2,32]{1,0:T(2,128)}, u32[]{:S(2)}) copy-start(f32[2,32]{1,0:T(2,128)} %param.19) | copy-start | bytes 772
  17.4 231.7 %all-gather.27.cloned.1.call-start = ((), (), s32[]{:S(2)}) async-start(), calls=%async_computation.29 | async-start | bytes 9461760 | tf_op jit(solution)/shard_map/all_gather | solution.py:234
  18.9 24.8 %all-to-all-start = ((bf16[4,128,1024]{2,1,0:T(8,128)(2,1)}), bf16[4,128,1024]{2,1,0:T(8,128)(2,1)S(1)}, u32[]{:S(2)}, u32[]{:S(2)}) async-start(bf16[4,128,1024]{2,1,0:T(8,128)(2,1)} %param.12), calls=%async_computation | async-start | bytes 2097152 | tf_op jit(solution)/shard_map/all_to_all | solution.py:281
  24.1 324.5 %all-gather.29.cloned.1.call-start = ((), (), s32[]{:S(2)}) async-start(), calls=%async_computation.30 | async-start | bytes 4325376 | tf_op jit(solution)/shard_map/all_gather | solution.py:234
  39.9 365.7 %copy-start.86 = (pred[256,256]{1,0:T(8,128)(4,1)}, pred[256,256]{1,0:T(8,128)(4,1)S(1)}, u32[]{:S(2)}) copy-start(pred[256,256]{1,0:T(8,128)(4,1)S(1)} %iota_compare_fusion) | copy-start | bytes 196612
  40.1 71.2 %copy-start.111 = (f32[2304]{0:T(1024)}, f32[2304]{0:T(1024)S(1)}, u32[]{:S(2)}) copy-start(f32[2304]{0:T(1024)S(1)} %reshape.652) | copy-start | bytes 27652
  40.3 71.1 %copy-start.112 = (f32[2304]{0:T(1024)}, f32[2304]{0:T(1024)S(1)}, u32[]{:S(2)}) copy-start(f32[2304]{0:T(1024)S(1)} %reshape.658) | copy-start | bytes 27652
  40.8 73.3 %copy-start.133 = (f32[1,256]{1,0:T(1,128)}, f32[1,256]{1,0:T(1,128)S(1)}, u32[]{:S(2)}) copy-start(f32[1,256]{1,0:T(1,128)S(1)} %get-tuple-element.219) | copy-start | bytes 3076
  40.9 73.3 %copy-start.135 = (f32[1,256]{1,0:T(1,128)}, f32[1,256]{1,0:T(1,128)S(1)}, u32[]{:S(2)}) copy-start(f32[1,256]{1,0:T(1,128)S(1)} %get-tuple-element.220) | copy-start | bytes 3076
  40.9 73.3 %copy-start.137 = (f32[1,256]{1,0:T(1,128)}, f32[1,256]{1,0:T(1,128)S(1)}, u32[]{:S(2)}) copy-start(f32[1,256]{1,0:T(1,128)S(1)} %get-tuple-element.221) | copy-start | bytes 3076
  40.9 73.3 %copy-start.139 = (f32[1,256]{1,0:T(1,128)}, f32[1,256]{1,0:T(1,128)S(1)}, u32[]{:S(2)}) copy-start(f32[1,256]{1,0:T(1,128)S(1)} %get-tuple-element.222) | copy-start | bytes 3076
  41.6 124.8 %copy-start.155 = (f32[16]{0:T(128)}, f32[16]{0:T(128)S(1)}, u32[]{:S(2)}) copy-start(f32[16]{0:T(128)S(1)} %get-tuple-element.244) | copy-start | bytes 196
  41.6 124.7 %copy-start.157 = (f32[16]{0:T(128)}, f32[16]{0:T(128)S(1)}, u32[]{:S(2)}) copy-start(f32[16]{0:T(128)S(1)} %get-tuple-element.245) | copy-start | bytes 196
  41.6 138.8 %copy-start.153 = (f32[16]{0:T(128)}, f32[16]{0:T(128)S(1)}, u32[]{:S(2)}) copy-start(f32[16]{0:T(128)S(1)} %get-tuple-element.246) | copy-start | bytes 196
  42.9 104.4 %copy-start.98 = (f32[1,1024]{1,0:T(1,128)}, f32[1,1024]{1,0:T(1,128)S(1)}, u32[]{:S(2)}) copy-start(f32[1,1024]{1,0:T(1,128)S(1)} %get-tuple-element.223) | copy-start | bytes 12292
  42.9 104.3 %copy-start.100 = (f32[1,1024]{1,0:T(1,128)}, f32[1,1024]{1,0:T(1,128)S(1)}, u32[]{:S(2)}) copy-start(f32[1,1024]{1,0:T(1,128)S(1)} %get-tuple-element.224) | copy-start | bytes 12292
  43.0 104.3 %copy-start.102 = (f32[1,1024]{1,0:T(1,128)}, f32[1,1024]{1,0:T(1,128)S(1)}, u32[]{:S(2)}) copy-start(f32[1,1024]{1,0:T(1,128)S(1)} %get-tuple-element.225) | copy-start | bytes 12292
  43.0 104.3 %copy-start.104 = (f32[1,1024]{1,0:T(1,128)}, f32[1,1024]{1,0:T(1,128)S(1)}, u32[]{:S(2)}) copy-start(f32[1,1024]{1,0:T(1,128)S(1)} %get-tuple-element.226) | copy-start | bytes 12292
  43.0 237.7 %copy-start.106 = (f32[1,1024]{1,0:T(1,128)}, f32[1,1024]{1,0:T(1,128)S(1)}, u32[]{:S(2)}) copy-start(f32[1,1024]{1,0:T(1,128)S(1)} %get-tuple-element.252) | copy-start | bytes 12292
  43.6 67.8 %copy-start.120 = (f32[1,4,256]{2,0,1:T(1,128)}, f32[1,4,256]{2,0,1:T(1,128)S(1)}, u32[]{:S(2)}) copy-start(f32[1,4,256]{2,0,1:T(1,128)S(1)} %get-tuple-element.230) | copy-start | bytes 12292
  43.6 205.5 %copy-start.122 = (f32[1,4,256]{2,0,1:T(1,128)}, f32[1,4,256]{2,0,1:T(1,128)S(1)}, u32[]{:S(2)}) copy-start(f32[1,4,256]{2,0,1:T(1,128)S(1)} %get-tuple-element.229) | copy-start | bytes 12292
  43.7 164.2 %copy-start.81 = (f32[1,4,512]{2,0,1:T(1,128)}, f32[1,4,512]{2,0,1:T(1,128)S(1)}, u32[]{:S(2)}) copy-start(f32[1,4,512]{2,0,1:T(1,128)S(1)} %get-tuple-element.228) | copy-start | bytes 24580
  43.7 312.9 %copy-start.65 = (f32[1,4,512]{2,0,1:T(1,128)}, f32[1,4,512]{2,0,1:T(1,128)S(1)}, u32[]{:S(2)}) copy-start(f32[1,4,512]{2,0,1:T(1,128)S(1)} %get-tuple-element.227) | copy-start | bytes 24580
  43.7 164.1 %copy-start.13 = (bf16[4,128,1024]{2,1,0:T(8,128)(2,1)}, bf16[4,128,1024]{2,1,0:T(8,128)(2,1)S(1)}, u32[]{:S(2)}) copy-start(bf16[4,128,1024]{2,1,0:T(8,128)(2,1)S(1)} %all-to-all-done) | copy-start | bytes 3145732
  44.0 67.4 %copy-start.113 = (f32[4,128]{1,0:T(4,128)}, f32[4,128]{1,0:T(4,128)S(1)}, u32[]{:S(2)}) copy-start(f32[4,128]{1,0:T(4,128)S(1)} %fusion.84) | copy-start | bytes 6148
  44.0 67.4 %copy-start.141 = (f32[4,128]{1,0:T(4,128)}, f32[4,128]{1,0:T(4,128)S(1)}, u32[]{:S(2)}) copy-start(f32[4,128]{1,0:T(4,128)S(1)} %fusion.170) | copy-start | bytes 6148
  213.9 43.2 %copy-start.7 = (f32[4,128,1024]{2,1,0:T(8,128)}, f32[4,128,1024]{2,1,0:T(8,128)S(1)}, u32[]{:S(2)}) copy-start(f32[4,128,1024]{2,1,0:T(8,128)S(1)} %get-tuple-element.238) | copy-start | bytes 6291460
  213.9 43.2 %copy-start.117 = (f32[4,128]{1,0:T(4,128)}, f32[4,128]{1,0:T(4,128)S(1)}, u32[]{:S(2)}) copy-start(f32[4,128]{1,0:T(4,128)S(1)} %get-tuple-element.237) | copy-start | bytes 6148
  213.9 43.2 %copy-start.144 = (f32[4,128]{1,0:T(4,128)}, f32[4,128]{1,0:T(4,128)S(1)}, u32[]{:S(2)}) copy-start(f32[4,128]{1,0:T(4,128)S(1)} %fusion.172) | copy-start | bytes 6148
  329.3 19.3 %all-to-all-start.6 = ((bf16[4,128,1024]{2,1,0:T(8,128)(2,1)}), bf16[4,128,1024]{2,1,0:T(8,128)(2,1)}, u32[]{:S(2)}, u32[]{:S(2)}) async-start(bf16[4,128,1024]{2,1,0:T(8,128)(2,1)} %param.22), calls=%async_computation.6 | async-start | bytes 2097152 | tf_op jit(solution)/shard_map/all_to_all | solution.py:282
  333.6 162.8 %reduce-scatter.19.cloned.1.call-start = ((), (), s32[]{:S(2)}) async-start(), calls=%async_computation.31 | async-start | bytes 884736
  342.4 14.2 slice-start.3
  384.4 14.0 copy-start.61
  384.4 14.0 copy-start.95
  438.9 238.2 %reduce-scatter.21.cloned.1.call-start = ((), (), s32[]{:S(2)}) async-start(), calls=%async_computation.32 | async-start | bytes 884736
  498.1 12.9 copy-start.24
  544.8 14.0 copy-start.15
  544.9 14.0 copy-start.59
  544.9 14.0 copy-start.93
  558.9 12.9 copy-start.43
  590.0 152.5 %reduce-scatter.17.cloned.1.call-start = ((), (), s32[]{:S(2)}) async-start(), calls=%async_computation.25 | async-start | bytes 4325376 | tf_op jit(solution)/shard_map/reduce_scatter | solution.py:243
  596.9 284.5 %reduce-scatter.15.cloned.1.call-start = ((), (), s32[]{:S(2)}) async-start(), calls=%async_computation.23 | async-start | bytes 4325376 | tf_op jit(solution)/shard_map/reduce_scatter | solution.py:243
  604.8 425.5 %reduce-scatter.13.cloned.1.call-start = ((), (), s32[]{:S(2)}) async-start(), calls=%async_computation.21 | async-start | bytes 9461760 | tf_op jit(solution)/shard_map/reduce_scatter | solution.py:243
  617.0 561.9 %reduce-scatter.11.cloned.1.call-start = ((), (), s32[]{:S(2)}) async-start(), calls=%async_computation.19 | async-start | bytes 9461760 | tf_op jit(solution)/shard_map/reduce_scatter | solution.py:243
  643.7 11.3 copy-start.99
  643.7 11.3 copy-start.101
  643.7 11.3 copy-start.103
  643.7 11.3 copy-start.105
  690.0 615.8 %all-reduce.54.cloned.1.call-start = ((), (), s32[]{:S(2)}) async-start(), calls=%async_computation.18 | async-start | bytes 235520 | tf_op jit(solution)/shard_map/psum | solution.py:464
  711.7 12.2 copy-start.83
  711.7 12.2 copy-start.165
  711.7 12.2 copy-start.166
  711.7 467.2 %copy-start.9 = (f32[4,128,1024]{2,1,0:T(8,128)S(1)}, f32[4,128,1024]{2,1,0:T(8,128)}, u32[]{:S(2)}) copy-start(f32[4,128,1024]{2,1,0:T(8,128)} %copy-done.7) | copy-start | bytes 6291460
  711.7 467.2 %copy-start.85 = (f32[4,128]{1,0:T(4,128)S(1)}, f32[4,128]{1,0:T(4,128)}, u32[]{:S(2)}) copy-start(f32[4,128]{1,0:T(4,128)} %copy-done.84) | copy-start | bytes 6148
  725.6 605.7 %all-gather.21.cloned.1.call-start = ((), (), s32[]{:S(2)}) async-start(), calls=%async_computation.26 | async-start | bytes 1179648 | tf_op jit(solution)/shard_map/all_gather | solution.py:244
  742.5 614.2 %all-gather.19.cloned.1.call-start = ((), (), s32[]{:S(2)}) async-start(), calls=%async_computation.24 | async-start | bytes 1179648 | tf_op jit(solution)/shard_map/all_gather | solution.py:244
  881.5 505.7 %all-gather.17.cloned.1.call-start = ((), (), s32[]{:S(2)}) async-start(), calls=%async_computation.22 | async-start | bytes 2580480 | tf_op jit(solution)/shard_map/all_gather | solution.py:244
  1030.3 387.4 %all-gather.15.cloned.1.call-start = ((), (), s32[]{:S(2)}) async-start(), calls=%async_computation.20 | async-start | bytes 2580480 | tf_op jit(solution)/shard_map/all_gather | solution.py:244
  1185.8 13.5 all-to-all-start.5
  1199.3 113.6 %all-to-all-start.11 = ((bf16[4,128,1024]{2,1,0:T(8,128)(2,1)}), bf16[4,128,1024]{2,1,0:T(8,128)(2,1)S(1)}, u32[]{:S(2)}, u32[]{:S(2)}) async-start(bf16[4,128,1024]{2,1,0:T(8,128)(2,1)} %fusion.83), calls=%async_computation.11 | async-start | bytes 2097152 | tf_op jit(solution)/shard_map/all_to_all | solution.py:483
  (156 other events, 825.9 us)
Sparse Core Ops, SparseCore 0:
  14.0 89.3 all-gather.22
  106.3 60.6 all-gather.24
  169.8 79.2 all-gather.26
  251.8 60.6 all-gather.28
  439.0 7.9 reduce-scatter.18
  590.1 7.9 reduce-scatter.20
  600.3 142.0 reduce-scatter.16
  744.7 136.6 reduce-scatter.14
  883.8 146.4 reduce-scatter.12
  1032.4 146.3 reduce-scatter.10
  1185.0 120.8 all-reduce.53
  1307.6 23.6 all-gather.20
  1333.2 23.4 all-gather.18
  1358.4 28.7 all-gather.16
  1388.9 28.7 all-gather.14
